TPU v7x, 256 devices: a whole 4x4x8 slice. The times are simulated.
256 devices in a mesh: dp: 16 (over z_hi, x, core), head: 16 (over z_lo, y).
Axes of the slice: x: 4, y: 4, z: 8 (z_hi: 2, z_lo: 4; z = z_hi * 4 + z_lo), core: 2. Of those that a mesh axis runs over, the one named last changes fastest.
Arguments:
- hidden: bfloat16 [8192, 1536], P('dp'), may hold values from -6 to 6
- token_prompt: int32 [8192], replicated, may hold values from 0 to 7, never falling along the last dimension, each value on 1 to 2048 neighbouring positions
- request_prompt: int32 [64], P('dp'), may hold values from 0 to 7
- in_gain: float32 [1536], replicated, may hold values from 0.1 to 1.9
- w_zx: float32 [1536, 2, 3072], P('dp', None, 'head'), may hold values from -0.15625 to 0.15625
- w_bc: float32 [1536, 256], P('dp'), may hold values from -0.0390625 to 0.0390625
- w_dt: float32 [1536, 48], P('dp', 'head'), may hold values from -0.15625 to 0.15625
- dt_bias: float32 [48], P('head'), may hold values from -3 to -0.5
- a_log: float32 [48], P('head'), may hold values from -9.5 to -1.6
- conv_x: float32 [4, 3072], P(None, 'head'), may hold values from -3 to 3
- conv_bc: float32 [4, 256], replicated, may hold values from -3 to 3
- skip_gain: float32 [48], P('head'), may hold values from 0.5 to 2
- out_gain: float32 [3072], P('head'), may hold values from 0.1 to 1.9
- w_out: bfloat16 [3072, 1536], P('head'), may hold values from -0.109375 to 0.109375
Outputs:
- layer_out: bfloat16 [8192, 1536], P(('dp', 'head'))
- request_states: float32 [64, 48, 64, 128], P('dp', 'head')
Inputs may be any that keep to these rules, and one draw needn't show every extreme that they name: `token_prompt`: prompt ids never fall along the tokens; each of the 8 prompts has at least one token.
All inputs are finite; a program needn't handle non-finite values.
Results may differ from a plain program's by a relative error of at most 0.012.
Values may be sent and summed in bfloat16 or wider, within the bound.
A program may use at most 64 MiB of HBM per device.

v0:
```python
import jax
import jax.numpy as jnp
from jax import lax
from jax.sharding import PartitionSpec as P

BLOCK = 256
PROMPTS = 8


EPSILON = 1e-05


def from_behind(shard, axis, by):
    peers = lax.axis_size(axis)
    pairs = [(i, i + by) for i in range(peers) if 0 <= i + by < peers]
    return lax.ppermute(shard, axis, pairs)


def carried_in(shard, axis, combine, identity):
    peers, position = (lax.axis_size(axis), lax.axis_index(axis))
    everything = jax.tree.map(lambda part: lax.all_gather(part, axis), shard)
    start = jax.tree.map(
        lambda part, zero: jnp.broadcast_to(jnp.asarray(zero, part.dtype), part.shape),
        shard,
        identity,
    )

    def step(k, before):
        reached = k < position
        new = combine(before, jax.tree.map(lambda part: part[k], everything))
        return jax.tree.map(lambda a, b: jnp.where(reached, a, b), new, before)

    return lax.fori_loop(0, peers, step, start)


def rms_scale(values):
    return lax.rsqrt(jnp.mean(values * values, axis=-1, keepdims=True) + EPSILON)


def conv_core(extended, extended_ids, token_ids, weights):
    length = token_ids.shape[0]
    total = jnp.zeros((length, extended.shape[1]), jnp.float32)
    for offset in range(weights.shape[0]):
        same = (extended_ids[offset : offset + length] == token_ids)[:, None]
        total = total + jnp.where(
            same, weights[offset] * extended[offset : offset + length].astype(jnp.float32), 0.0
        )
    return jax.nn.silu(total).astype(jnp.bfloat16)


def block_local(x_blk, b_blk, c_blk, step_blk, rate_blk, ids_blk, before_id):
    length = ids_blk.shape[0]
    position = jnp.arange(length, dtype=jnp.int32)
    prefix = jnp.cumsum(rate_blk, axis=0)
    prefix_t = prefix.T
    same = (ids_blk[:, None] == ids_blk[None, :]) & (position[None, :] <= position[:, None])
    gaps = prefix_t[:, :, None] - prefix_t[:, None, :]
    decay = jnp.where(same[None], jnp.exp(jnp.where(same[None], gaps, 0.0)), 0.0)
    scores = jnp.dot(c_blk, b_blk.T, preferred_element_type=jnp.float32)
    mixing = (scores[None] * decay * step_blk.T[:, None, :]).astype(jnp.bfloat16)
    y_intra = jnp.einsum("hts,shp->thp", mixing, x_blk, preferred_element_type=jnp.float32)
    end_id = ids_blk[-1]
    alive = ids_blk == end_id
    weight_end = (
        jnp.where(
            alive[None, :],
            jnp.exp(jnp.where(alive[None, :], prefix_t[:, -1:] - prefix_t, 0.0)),
            0.0,
        )
        * step_blk.T
    )
    b_weighted = (weight_end[:, :, None] * b_blk[None]).astype(jnp.bfloat16)
    local_state = jnp.einsum("hsn,shp->hpn", b_weighted, x_blk, preferred_element_type=jnp.float32)
    carry_gain = jnp.where(end_id == before_id, jnp.exp(prefix_t[:, -1]), 0.0)
    return (y_intra, local_state, carry_gain, prefix)


def block_inter(c_blk, prefix, ids_blk, before_id, state_in):
    entering = ids_blk == before_id
    inter_scale = jnp.where(entering[:, None], jnp.exp(prefix), 0.0)
    return inter_scale[:, :, None] * jnp.einsum(
        "tn,hpn->thp", c_blk.astype(jnp.float32), state_in, precision=lax.Precision.HIGHEST
    )


def block_last(
    last_index, table, x_blk, b_blk, step_blk, prefix, ids_blk, before_id, state_in, start
):
    length = ids_blk.shape[0]
    position = jnp.arange(length, dtype=jnp.int32)
    prompt_ids = jnp.arange(last_index.shape[0], dtype=jnp.int32)
    local_last = last_index - start
    ends_here = (local_last >= 0) & (local_last < length)
    clipped = jnp.clip(local_last, 0, length - 1)

    def with_ends():
        prefix_t = prefix.T
        prefix_last = prefix[clipped]
        pick = (
            ends_here[:, None]
            & (ids_blk[None, :] == prompt_ids[:, None])
            & (position[None, :] <= clipped[:, None])
        )
        spans = prefix_last[:, :, None] - prefix_t[None]
        weight_last = (
            jnp.where(pick[:, None, :], jnp.exp(jnp.where(pick[:, None, :], spans, 0.0)), 0.0)
            * step_blk.T[None]
        )
        b_last = (weight_last[..., None] * b_blk[None, None]).astype(jnp.bfloat16)
        last_local = jnp.einsum("ghsn,shp->ghpn", b_last, x_blk, preferred_element_type=jnp.float32)
        last_gain = jnp.where(
            (ends_here & (prompt_ids == before_id))[:, None], jnp.exp(prefix_last), 0.0
        )
        return table + last_local + last_gain[:, :, None, None] * state_in[None]

    def without_ends():
        return table

    return lax.cond(jnp.any(ends_here), with_ends, without_ends)


def join_states(earlier, later):
    return (earlier[0] * later[0], later[0][:, None, None] * earlier[1] + later[1])


def on_device(
    hidden,
    token_prompt,
    request_prompt,
    in_gain,
    w_zx,
    w_bc,
    w_dt,
    dt_bias,
    a_log,
    conv_x,
    conv_bc,
    skip_gain,
    out_gain,
    w_out,
):
    tok_dev = hidden.shape[0]
    inner_dev = w_zx.shape[2]
    heads_dev = w_dt.shape[1]
    head_dim = inner_dev // heads_dev
    state_width = w_bc.shape[1] // 2
    taps = conv_x.shape[0]
    dp_index = lax.axis_index("dp")
    head_index = lax.axis_index("head")
    head_count = lax.axis_size("head")
    hidden_f = hidden.astype(jnp.float32)
    normed = (hidden_f * rms_scale(hidden_f) * in_gain).astype(jnp.bfloat16)
    pieces = (
        lax.all_gather(w_zx.astype(jnp.bfloat16), "dp", axis=0, tiled=True),
        lax.all_gather(w_dt.astype(jnp.bfloat16), "dp", axis=0, tiled=True),
        lax.all_gather(w_bc.astype(jnp.bfloat16), "dp", axis=0, tiled=True),
    )
    acc_zx, acc_step, acc_bc = tuple(
        (
            jnp.dot(normed, piece.reshape(piece.shape[0], -1), preferred_element_type=jnp.float32)
            for piece in pieces
        )
    )
    proj_bc = acc_bc.astype(jnp.bfloat16)
    proj_zx = acc_zx.astype(jnp.bfloat16)
    gate_z = proj_zx[:, :inner_dev]
    inner_x = proj_zx[:, inner_dev:]
    proj_dt = acc_step.astype(jnp.bfloat16)
    step_size = jax.nn.softplus(proj_dt.astype(jnp.float32) + dt_bias)
    rate = step_size * -jnp.exp(a_log)
    ids_own = lax.dynamic_slice_in_dim(token_prompt, dp_index * tok_dev, tok_dev)
    rim_start = jnp.maximum(dp_index * tok_dev - (taps - 1), 0)
    rim_ids = lax.dynamic_slice_in_dim(token_prompt, rim_start, taps - 1)
    tail_rows = jnp.concatenate(
        [inner_x[tok_dev - taps + 1 :], proj_bc[tok_dev - taps + 1 :]], axis=1
    )
    rim_rows = from_behind(tail_rows, "dp", 1)
    ext_ids = jnp.concatenate([rim_ids, ids_own])
    conv_inner = conv_core(
        jnp.concatenate([rim_rows[:, :inner_dev], inner_x], axis=0), ext_ids, ids_own, conv_x
    )
    conv_bc_out = conv_core(
        jnp.concatenate([rim_rows[:, inner_dev:], proj_bc], axis=0), ext_ids, ids_own, conv_bc
    )
    blocks = tok_dev // BLOCK
    x_heads = conv_inner.reshape(blocks, BLOCK, heads_dev, head_dim)
    b_conv = conv_bc_out[:, :state_width].reshape(blocks, BLOCK, state_width)
    c_conv = conv_bc_out[:, state_width:].reshape(blocks, BLOCK, state_width)
    step_blocks = step_size.reshape(blocks, BLOCK, heads_dev)
    rate_blocks = rate.reshape(blocks, BLOCK, heads_dev)
    id_blocks = ids_own.reshape(blocks, BLOCK)
    prev_last = jnp.where(dp_index > 0, token_prompt[jnp.maximum(dp_index * tok_dev - 1, 0)], -1)
    before_ids = jnp.concatenate([prev_last[None], id_blocks[:-1, -1]])
    y_intra, local_state, carry_gain, prefix = jax.vmap(block_local)(
        x_heads, b_conv, c_conv, step_blocks, rate_blocks, id_blocks, before_ids
    )

    def advance(carry, item):
        gain_acc, state_acc = carry
        gain, block_state = item
        return (
            (gain_acc * gain, gain[:, None, None] * state_acc + block_state),
            (gain_acc, state_acc),
        )

    unit_gain = jnp.ones((heads_dev,), jnp.float32)
    zero_state = jnp.zeros((heads_dev, head_dim, state_width), jnp.float32)
    (dev_gain, dev_state), (prior_gain, prior_state) = lax.scan(
        advance, (unit_gain, zero_state), (carry_gain, local_state)
    )
    scanned = carried_in((dev_gain, dev_state), "dp", join_states, (unit_gain, zero_state))
    incoming = scanned[1]
    block_in = prior_state + prior_gain[:, :, None, None] * incoming[None]
    prompt_ids = jnp.arange(PROMPTS, dtype=jnp.int32)
    last_index = (
        jnp.sum((token_prompt[None, :] <= prompt_ids[:, None]).astype(jnp.int32), axis=1) - 1
    )
    start_pos = (dp_index * blocks + jnp.arange(blocks, dtype=jnp.int32)) * BLOCK
    y_inter = jax.vmap(block_inter)(c_conv, prefix, id_blocks, before_ids, block_in)

    def collect(table, item):
        xb, bb, sb, pb, ib, fb, stb, ob = item
        return (block_last(last_index, table, xb, bb, sb, pb, ib, fb, stb, ob), None)

    empty_table = jnp.zeros((PROMPTS, heads_dev, head_dim, state_width), jnp.float32)
    local_table, unused = lax.scan(
        collect,
        empty_table,
        (x_heads, b_conv, step_blocks, prefix, id_blocks, before_ids, block_in, start_pos),
    )
    ssd_out = (y_intra + y_inter).reshape(tok_dev, heads_dev, head_dim) + skip_gain[
        None, :, None
    ] * conv_inner.astype(jnp.float32).reshape(tok_dev, heads_dev, head_dim)
    gated = ssd_out.reshape(tok_dev, inner_dev) * jax.nn.silu(gate_z.astype(jnp.float32))
    square_sum = lax.psum(jnp.sum(gated * gated, axis=1), "head")
    scale = lax.rsqrt(square_sum / (inner_dev * head_count) + EPSILON)
    normed_out = (gated * scale[:, None] * out_gain).astype(jnp.bfloat16)
    out_rows = tok_dev // head_count
    own_rows = lax.dynamic_slice_in_dim(hidden_f, head_index * out_rows, out_rows, 0)
    mixed = lax.psum_scatter(
        jnp.dot(normed_out, w_out, preferred_element_type=jnp.float32),
        "head",
        scatter_dimension=0,
        tiled=True,
    )
    layer_out = (own_rows + mixed).astype(jnp.bfloat16)
    table = lax.psum(local_table, "dp")
    one_hot = (request_prompt[:, None] == prompt_ids[None, :]).astype(jnp.float32)
    request_states = jnp.einsum("rg,ghpn->rhpn", one_hot, table, precision=lax.Precision.HIGHEST)
    return (layer_out, request_states)


def solution(mesh):
    in_specs = (
        P("dp", None),
        P(),
        P("dp"),
        P(),
        P("dp", None, "head"),
        P("dp", None),
        P("dp", "head"),
        P("head"),
        P("head"),
        P(None, "head"),
        P(),
        P("head"),
        P("head"),
        P("head", None),
    )
    out_specs = (P(("dp", "head"), None), P("dp", "head", None, None))
    return jax.shard_map(
        on_device, mesh=mesh, in_specs=in_specs, out_specs=out_specs, check_vma=False
    )
```

profile of v0, /device:TPU:2, one launch (start us, length us, event | category | flops | bytes accessed | tf_op | source)
XLA Modules:
  0.0 481.3 jit_solution(6186627357808933875)
XLA Ops:
  7.3 1.8 convert_element_type.107
  14.0 1.8 multiply_reduce_fusion
  15.8 26.4 %all-gather.2 = bf16[16,96,3]{1,2,0:T(4,128)(2,1)S(1)} all-gather(bf16[1,96,3]{1,2,0:T(4,128)(2,1)S(1)} %convert_bitcast_fusion), channel_id=1, replica_groups=mesh['dp'=16,'head'=16] {'dp'}, dimensions={0}, use_global_device_ids=true | all-gather | bytes 9792 | tf_op jit(solution)/shard_map/all_gather | solution.py:155
  43.1 1.8 reduce-window.6
  45.7 35.6 %all_gather.22 = bf16[1536,256]{1,0:T(8,128)(2,1)S(1)} all-gather(bf16[96,256]{1,0:T(8,128)(2,1)S(1)} %convert_element_type.109), channel_id=1, replica_groups=mesh['dp'=16,'head'=16] {'dp'}, dimensions={0}, use_global_device_ids=true | all-gather | bytes 835584 | tf_op jit(solution)/shard_map/all_gather | solution.py:156
  85.7 1.3 slice_compare_fusion.2
  89.0 3.5 copy.98
  94.3 2.4 collective-permute-start
  97.5 4.9 %collective-permute-done = bf16[3,448]{0,1:T(8,128)(2,1)S(1)} collective-permute-done((bf16[3,448]{0,1:T(8,128)(2,1)S(1)}, bf16[3,448]{0,1:T(8,128)(2,1)S(1)}, u32[]{:S(2)}, u32[]{:S(2)}) %collective-permute-start) | collective-permute-done | bytes 2720 | tf_op jit(solution)/shard_map/ppermute | solution.py:16
  102.5 2.1 multiply_convert_fusion.12
  112.9 34.7 %all-reduce = f32[48]{0:T(128)S(1)} all-reduce(f32[48]{0:T(128)S(1)} %dynamic-update-slice), channel_id=2, replica_groups=mesh['dp'=16,'head'=16] {'dp'}, use_global_device_ids=true, to_apply=%add | all-reduce | flops 48 | bytes 384
  149.8 20.3 %all-gather.8.cloned.1.call-done = f32[48,64,128]{2,1,0:T(8,128)} async-done(((f32[3,64,128]{2,1,0:T(8,128)}), f32[48,64,128]{2,1,0:T(8,128)}) %all-gather.8.cloned.1.call-update) | async-done | bytes 1572880 | tf_op jit(solution)/shard_map/all_gather | solution.py:21
  170.1 16.3 %while.49 = (s32[]{:T(128)}, f32[3,64,128]{2,1,0:T(8,128)S(1)}, s32[]{:T(128)}, f32[16,3]{1,0:T(8,128)S(1)}, f32[16,3,64,128]{3,2,1,0:T(8,128)}) while((s32[]{:T(128)}, f32[3,64,128]{2,1,0:T(8,128)S(1)}, s32[]{:T(128)}, f32[16,3]{1,0:T(8,128)S(1)}, f32[16,3,64,128]{3,2,1,0:T(8,128)}) %tuple.140), condition=%wide.region_6.7_spmd.clone.clone, body=%wide.region_5.6_spmd.clone.sunk.clone | while | flops 98308 | bytes 295045 | solution.py:33
  189.7 12.3 %while.47 = (s32[]{:T(128)}, f32[8,3,64,128]{3,2,0,1:T(8,128)S(1)}, s32[2]{0:T(128)S(1)}, s32[8]{0:T(128)S(1)}, s32[2,256]{1,0:T(2,128)S(1)}, /*index=5*/f32[2,2...) while((s32[]{:T(128)}, f32[8,3,64,128]{3,2,0,1:T(8,128)S(1)}, ...), condition=%wide.region_15.16_spmd.clone, body=%wide.region_11.15_spmd.sunk.clone | while | flops 102892680 | bytes 2386139 | solution.py:226
  192.2 7.2 %conditional.3 = (f32[8,3,64,128]{3,2,0,1:T(8,128)S(1)}) conditional(s32[]{:T(128)} %convert_element_type.204, f32[8,3,64,128]{3,2,0,1:T(8,128)S(1)} %get-tuple-element.774, (pred[8]{0:T(512)(128)(4,1)S(1)}, s32[2,256]{1,0:T(2,128)S(1)}, s32[]{:T(128)}, s32[8]{0:T(128)S(1)}, s32[256]{0:T(256)S(1)}, /*index=5*/s32[8]{0:T(128)S(1)}, ...), branch_computations={%region_13.13_spmd, %region_14.14_spmd} | conditional | flops 102892616 | bytes 2384684 | solution.py:119
  197.3 2.1 fusion.5
  202.0 1.3 copy.123
  204.6 41.1 %psum.14 = f32[512]{0:T(512)S(1)} all-reduce(f32[512]{0:T(512)S(1)} %get-tuple-element.491), channel_id=1, replica_groups=mesh['dp'=16,'head'=16] {'head'}, use_global_device_ids=true, to_apply=%region_8.9 | all-reduce | flops 512 | bytes 4096 | tf_op jit(solution)/shard_map/psum | solution.py:235
  245.7 2.3 fusion.34
  248.0 2.1 convert_element_type.105
  250.1 120.9 %all-reduce.3.cloned.1.call-done = f32[8,3,64,128]{3,0,2,1:T(8,128)} async-done(((f32[8,3,64,128]{3,0,2,1:T(8,128)}), f32[8,3,64,128]{3,0,2,1:T(8,128)}) %all-reduce.3.cloned.1.call-update) | async-done | bytes 786448 | tf_op jit(solution)/shard_map/psum | solution.py:247
  371.0 1.6 fusion.42
  373.4 99.7 %reduce-scatter.2.cloned.1.call-done = f32[32,1536]{1,0:T(8,128)} async-done(((f32[512,1536]{1,0:T(8,128)}), f32[32,1536]{1,0:T(8,128)}) %reduce-scatter.2.cloned.1.call-update) | async-done | bytes 196624 | tf_op jit(solution)/shard_map/reduce_scatter | solution.py:240
  473.1 1.7 add_convert_fusion
  (218 shorter events, 54.4 us)
Async XLA Ops:
  7.2 238.5 %copy-start = (bf16[192,1536]{1,0:T(8,128)(2,1)S(1)}, bf16[192,1536]{1,0:T(8,128)(2,1)}, u32[]{:S(2)}) copy-start(bf16[192,1536]{1,0:T(8,128)(2,1)} %param.35) | copy-start | bytes 1769476
  7.2 35.2 %copy-start.2 = (bf16[512,1536]{1,0:T(8,128)(2,1)S(1)}, bf16[512,1536]{1,0:T(8,128)(2,1)}, u32[]{:S(2)}) copy-start(bf16[512,1536]{1,0:T(8,128)(2,1)} %param.22) | copy-start | bytes 4718596
  7.2 35.2 %copy-start.23 = (f32[1536]{0:T(1024)S(1)}, f32[1536]{0:T(1024)}, u32[]{:S(2)}) copy-start(f32[1536]{0:T(1024)} %param.25) | copy-start | bytes 18436
  7.2 35.2 %copy-start.25 = (f32[3]{0:T(128)S(1)}, f32[3]{0:T(128)}, u32[]{:S(2)}) copy-start(f32[3]{0:T(128)} %param.29) | copy-start | bytes 40
  7.2 81.7 %all-gather.6.cloned.1.call-start = ((), (), s32[]{:S(2)}) async-start(), calls=%async_computation.1 | async-start | bytes 1671168 | tf_op jit(solution)/shard_map/all_gather | solution.py:154
  9.1 161.1 %all-gather.8.cloned.1.call-start = ((), (), s32[]{:S(2)}) async-start(), calls=%async_computation.4 | async-start | bytes 1671168 | tf_op jit(solution)/shard_map/all_gather | solution.py:21
  15.8 65.4 %copy-start.16 = (f32[512]{0:T(512)}, f32[512]{0:T(512)S(1)}, u32[]{:S(2)}) copy-start(f32[512]{0:T(512)S(1)} %add_rsqrt_fusion.1) | copy-start | bytes 6148
  42.4 3.2 copy-start.8
  81.2 5.8 %copy-start.10 = (f32[4,192]{1,0:T(4,128)S(1)}, f32[4,192]{1,0:T(4,128)}, u32[]{:S(2)}) copy-start(f32[4,192]{1,0:T(4,128)} %param.31) | copy-start | bytes 9220
  81.2 6.4 %copy-start.11 = (f32[4,256]{1,0:T(4,128)S(1)}, f32[4,256]{1,0:T(4,128)}, u32[]{:S(2)}) copy-start(f32[4,256]{1,0:T(4,128)} %param.32) | copy-start | bytes 12292
  82.7 9.8 %copy-start.17 = (f32[512]{0:T(512)S(1)}, f32[512]{0:T(512)}, u32[]{:S(2)}) copy-start(f32[512]{0:T(512)} %copy-done.16) | copy-start | bytes 6148
  82.7 9.8 %copy-start.24 = (f32[1536]{0:T(1024)S(1)}, f32[1536]{0:T(1024)}, u32[]{:S(2)}) copy-start(f32[1536]{0:T(1024)} %param.25) | copy-start | bytes 18436
  85.1 8.4 %copy-start.13 = (s32[2]{0:T(128)}, s32[2]{0:T(128)S(1)}, u32[]{:S(2)}) copy-start(s32[2]{0:T(128)S(1)} %get-tuple-element.771) | copy-start | bytes 28
  92.5 4.2 copy-start.15
  94.3 10.5 %slice-start = ((bf16[512,384]{0,1:T(8,128)(2,1)}), bf16[512,192]{0,1:T(8,128)(2,1)S(1)}, s32[]{:S(2)}) async-start(bf16[512,384]{0,1:T(8,128)(2,1)} %copy-done.6), calls=%async_computation.5 | async-start | bytes 393216 | tf_op jit(solution)/shard_map/slice | solution.py:167
  94.3 8.1 %collective-permute-start = (bf16[3,448]{0,1:T(8,128)(2,1)S(1)}, bf16[3,448]{0,1:T(8,128)(2,1)S(1)}, u32[]{:S(2)}, u32[]{:S(2)}) collective-permute-start(bf16[3,448]{0,1:T(8,128)(2,1)S(1)} %pad_maximum_fusion.2), channel_id=1, source_target_pairs={{0,16},{16,32},{32,48},{48,64},{64,80},{80,96},{96,112},{112,128},... | collective-permute-start | bytes 8072 | tf_op jit(solution)/shard_map/ppermute | solution.py:16
  107.2 2.2 copy-start.26
  107.2 3.6 copy-start.9
  108.2 262.8 %all-reduce.3.cloned.1.call-start = ((), (), s32[]{:S(2)}) async-start(), calls=%async_computation.3 | async-start | bytes 1572864 | tf_op jit(solution)/shard_map/psum | solution.py:247
  149.8 36.7 %copy-start.19 = (f32[2,3]{1,0:T(2,128)S(1)}, f32[2,3]{1,0:T(2,128)}, u32[]{:S(2)}) copy-start(f32[2,3]{1,0:T(2,128)} %copy-done.18) | copy-start | bytes 76
  187.3 2.4 copy-start.14
  202.0 43.7 %copy-start.20 = (f32[192]{0:T(256)S(1)}, f32[192]{0:T(256)}, u32[]{:S(2)}) copy-start(f32[192]{0:T(256)} %param.34) | copy-start | bytes 2308
  203.4 269.8 %reduce-scatter.2.cloned.1.call-start = ((), (), s32[]{:S(2)}) async-start(), calls=%async_computation.2 | async-start | bytes 3342336 | tf_op jit(solution)/shard_map/reduce_scatter | solution.py:240
  248.0 123.0 %copy-start.21 = (s32[4]{0:T(128)S(1)}, s32[4]{0:T(128)}, u32[]{:S(2)}) copy-start(s32[4]{0:T(128)} %param.24) | copy-start | bytes 52
  (9 other events, 9.1 us)
Sparse Core Ops, SparseCore 0:
  11.4 60.7 all-gather.5
  108.3 61.7 all-gather.7
  203.5 167.4 all-reduce.2
  373.6 99.4 reduce-scatter.1
where the time goes:
time: 483 us; the launch traced here: 481 us
  waiting for transfers between devices  246 us (51%)
  blocking collectives  138 us (29%)
  other arithmetic  40.5 us (8%)
  local copies, waits for them, and re-layouts  24.7 us (5%)
  between operations  15.7 us (3%)
  matrix products  12.1 us (3%)
    psum x1, waiting for transfers between devices, on_device(): table = lax.psum(local_table, 'dp')  121 us
    reduce_scatter x1, waiting for transfers between devices, on_device(): lax.psum_scatter(jnp.dot(normed_out, w_out, preferred_element_type=jnp.fl...  99.7 us
    psum x1, blocking collectives, on_device(): square_sum = lax.psum(jnp.sum(gated * gated, axis=1), 'head')  41.1 us
    all_gather x1, blocking collectives, on_device(): lax.all_gather(w_bc.astype(jnp.bfloat16), 'dp', axis=0, tiled=True)  35.6 us
    unnamed x1, blocking collectives  34.7 us
    all_gather x1, blocking collectives, on_device(): lax.all_gather(w_dt.astype(jnp.bfloat16), 'dp', axis=0, tiled=True)  26.4 us
    all_gather x1, waiting for transfers between devices, carried_in(): everything = jax.tree.map(lambda part: lax.all_gather(part, axis), shard)  20.3 us
    select_n x16, other arithmetic, step(): return jax.tree.map(lambda a, b: jnp.where(reached, a, b), new, before)  15.7 us
  transfers between devices with their start and end apart: 5, of which 4 were waited for; matrix products, arithmetic and copies ran while one was open for 6% of the time, Pallas kernels for 0%

commit v1 on v0

v1 whole, which is shorter than its diff:
```python
import jax
import jax.numpy as jnp
from jax import lax
from jax.experimental import pallas as pl
from jax.experimental.pallas import tpu as pltpu
from jax.sharding import PartitionSpec as P

MESH = pl.DeviceIdType.MESH
F32 = jnp.float32
BF16 = jnp.bfloat16
EPSILON = 1e-05

DP = 16
HD = 16
D = 1536
TOK = 512
EXT = TOK + 16
ROWS = 96
HEADS = 3
FEAT = 192
NSTATE = 128
PROMPTS = 8
OUTW = D + 128

W_IDS = 0
T_IDS = 15
F_IDS = 30
HALO = 45
INFO_UP = 46
INFO_DN = 50
STATE = 54
WO_UP = 58
WO_DN = 64
WO_UPP = 70
WO_DNP = 76
TAB0 = 82
TABZ = 83
TABX = 84
A2A = 87
RSY = 90
N_MSG = 93


def dot(a, b):
    return lax.dot_general(a, b, (((1,), (0,)), ((), ())), preferred_element_type=F32)


def dot_t(a, b):
    return lax.dot_general(a, b, (((1,), (1,)), ((), ())), preferred_element_type=F32)


def lane_cumsum(v):
    width = v.shape[1]
    lane = lax.broadcasted_iota(jnp.int32, v.shape, 1)
    step = 1
    while step < width:
        v = v + jnp.where(lane >= step, pltpu.roll(v, step, 1), 0.0)
        step *= 2
    return v


def run_end(v, ids):
    width = v.shape[1]
    lane = lax.broadcasted_iota(jnp.int32, v.shape, 1)
    step = 1
    while step < width:
        same = (pltpu.roll(ids, width - step, 1) == ids) & (lane < width - step)
        v = jnp.where(same, pltpu.roll(v, width - step, 1), v)
        step *= 2
    return v


def body(
    ids_ref, req_ref, dtb_ref, alog_ref, skip_ref, hid_ref, gain_ref, wzx_ref, wbc_ref,
    wdt_ref, cx_ref, cbc_ref, og_ref, wout_ref, out_ref, st_ref,
    w_buf, wst, wdt_all, wdt_mat, halo, nrm, idc, u_buf, taps, x_t, x_b, b_b, c_b, b_all,
    info_tx, info_rx, l_tx, l_rx, s_in, cols, smask, loc, tab0, tabs, tabz, tabm, tabx, fin,
    g_send, a_rx, wo, part, own_acc, rs_rx, send_sem, recv_sem, local_sem,
):
    dp = lax.axis_index("dp")
    hd = lax.axis_index("head")
    zh = dp // 8
    x = (dp // 2) % 4
    c = dp % 2
    zl = hd // 4
    y = hd % 4
    sgn = 1 - 2 * c

    def dev(z_, x_, c_):
        return z_ * 8 + lax.rem(x_ + 8, 4) * 2 + c_

    ahead = dev(zh, x + sgn, c)
    behind = dev(zh, x - sgn, c)
    across = dev(1 - zh, x, c)
    mate = dev(zh, x, 1 - c)

    def dpid(d):
        return {"dp": d}

    def hdid(z_, y_):
        return {"head": z_ * 4 + y_}

    def msg(m, src, dst, to):
        return pltpu.make_async_remote_copy(
            src_ref=src, dst_ref=dst, send_sem=send_sem.at[m], recv_sem=recv_sem.at[m],
            device_id=to, device_id_type=MESH,
        )

    pending = []

    def send(m, src, dst, to, cond=None):
        if cond is None:
            msg(m, src, dst, to).start()
        else:
            @pl.when(cond)
            def _():
                msg(m, src, dst, to).start()
        pending.append((m, src, dst, to, cond))

    def recv(m, dst, to, cond=None):
        if cond is None:
            msg(m, dst, dst, to).wait_recv()
        else:
            @pl.when(cond)
            def _():
                msg(m, dst, dst, to).wait_recv()

    class Gather:
        def __init__(self, families):
            self.families = families

        def send(self, k, owner, to):
            for base, ref_of in self.families:
                r = ref_of(owner)
                send(base + k, r, r, dpid(to))

        def recv(self, k, owner):
            for base, ref_of in self.families:
                recv(base + k, ref_of(owner), dpid(mate))

        def own(self):
            self.send(3, dp, across)
            self.send(0, dp, ahead)
            self.send(1, dp, behind)
            self.send(7, dp, mate)

        def near(self):
            self.recv(0, dev(zh, x - sgn, c))
            self.send(2, dev(zh, x - sgn, c), ahead)
            self.send(8, dev(zh, x - sgn, c), mate)
            self.recv(1, dev(zh, x + sgn, c))
            self.send(9, dev(zh, x + sgn, c), mate)

        def cross(self):
            self.recv(3, dev(1 - zh, x, c))
            self.send(4, dev(1 - zh, x, c), ahead)
            self.send(5, dev(1 - zh, x, c), behind)
            self.send(11, dev(1 - zh, x, c), mate)

        def near_rest(self):
            self.recv(2, dev(zh, x + 2, c))
            self.send(10, dev(zh, x + 2, c), mate)
            self.recv(7, dev(zh, x, 1 - c))
            self.recv(8, dev(zh, x + sgn, 1 - c))
            self.recv(9, dev(zh, x - sgn, 1 - c))
            self.recv(10, dev(zh, x + 2, 1 - c))

        def far(self):
            o = 1 - zh
            self.recv(4, dev(o, x - sgn, c))
            self.send(6, dev(o, x - sgn, c), ahead)
            self.send(12, dev(o, x - sgn, c), mate)
            self.recv(5, dev(o, x + sgn, c))
            self.send(13, dev(o, x + sgn, c), mate)
            self.recv(6, dev(o, x + 2, c))
            self.send(14, dev(o, x + 2, c), mate)
            self.recv(11, dev(o, x, 1 - c))
            self.recv(12, dev(o, x + sgn, 1 - c))
            self.recv(13, dev(o, x - sgn, 1 - c))
            self.recv(14, dev(o, x + 2, 1 - c))

    barrier = pltpu.get_barrier_semaphore()
    for k in range(1, DP):
        pl.semaphore_signal(
            barrier, inc=1, device_id=dpid(lax.rem(dp + k, DP)), device_id_type=MESH
        )
    for k in range(1, 4):
        pl.semaphore_signal(
            barrier, inc=1, device_id=hdid(zl, lax.rem(y + k, 4)), device_id_type=MESH
        )
        pl.semaphore_signal(
            barrier, inc=1, device_id=hdid(lax.rem(zl + k, 4), y), device_id_type=MESH
        )

    zw = wzx_ref[:, 0, :]
    xw = wzx_ref[:, 1, :]
    wst[:, 0:128] = xw[:, 0:128]
    wst[:, 128:256] = jnp.concatenate([xw[:, 128:192], zw[:, 128:192]], axis=1)
    wst[:, 256:384] = zw[:, 0:128]
    wst[:, 384:640] = wbc_ref[...]
    own_rows = pl.multiple_of(dp * ROWS, ROWS)
    w_buf[pl.ds(own_rows, ROWS), :] = wst[...].astype(BF16)
    wdt_pad = jnp.concatenate(
        [
            jnp.concatenate([wdt_ref[...], jnp.zeros((ROWS, 125), F32)], axis=1),
            jnp.zeros((32, 128), F32),
        ],
        axis=0,
    )
    wdt_all[dp] = wdt_pad.T[0:8, :]

    def w_rows(owner):
        return w_buf.at[pl.ds(pl.multiple_of(owner * ROWS, ROWS), ROWS), :]

    def t_rows(owner):
        return wdt_all.at[owner]

    weights = Gather([(W_IDS, w_rows), (T_IDS, t_rows)])
    own_copy = pltpu.make_async_copy(wout_ref, wo.at[zl], local_sem)
    own_copy.start()

    @pl.when(dp == 0)
    def _():
        halo[...] = jnp.zeros_like(halo)

    for j in range(4):
        @pl.when(dp < j + 1)
        def _():
            info_rx[j] = jnp.zeros((16, 128), F32)
            l_rx[j] = jnp.zeros((FEAT, NSTATE), BF16)

        @pl.when(dp + j + 1 > DP - 1)
        def _():
            info_rx[4 + j] = jnp.zeros((16, 128), F32)

    pl.semaphore_wait(barrier, DP - 1 + 6)

    weights.own()
    send(HALO, hid_ref.at[pl.ds(TOK - 16, 16), :], halo, dpid(lax.rem(dp + 1, DP)), dp < DP - 1)

    own_ids = ids_ref[dp].astype(F32)
    prev_ids = ids_ref[jnp.maximum(dp - 1, 0)].astype(F32)
    prev_col = jnp.broadcast_to(prev_ids[3:4, :], (128, 128)).T[112:128, :]
    first_dev = jnp.zeros((16, 128), jnp.int32) + dp == 0
    idc[0:16, :] = jnp.where(first_dev, -1.0, prev_col)
    for q in range(4):
        idc[16 + 128 * q : 144 + 128 * q, :] = jnp.broadcast_to(own_ids[q : q + 1, :], (128, 128)).T
    id_row = jnp.concatenate([own_ids[q : q + 1, :] for q in range(4)], axis=1)

    taps[...] = jnp.zeros_like(taps)
    taps[0:4, 0:128] = cx_ref[:, 0:128]
    taps[0:4, 128:192] = cx_ref[:, 128:192]
    taps[0:4, 256:512] = cbc_ref[...]

    gain = gain_ref[...]

    def norm_rows(rows):
        h = rows.astype(F32)
        scale = lax.rsqrt(jnp.mean(h * h, axis=1, keepdims=True) + EPSILON)
        return (h * scale * gain).astype(BF16)

    def norm_step(i, carry):
        r = pl.multiple_of(i * 32, 32)
        nrm[pl.ds(pl.multiple_of(16 + r, 16), 32), :] = norm_rows(hid_ref[pl.ds(r, 32), :])
        return carry

    lax.fori_loop(0, TOK // 32, norm_step, 0)
    recv(HALO, halo, dpid(mate), dp > 0)
    nrm[0:16, :] = norm_rows(halo[...])

    half = pl.multiple_of(c * 96, 96)

    def wo_rows(z_):
        return wo.at[jnp.clip(z_, 0, 3), pl.ds(half, 96), :]

    def wo_mate_rows(z_):
        return wo.at[jnp.clip(z_, 0, 3), pl.ds(pl.multiple_of((1 - c) * 96, 96), 96), :]

    def wo_start():
        send(WO_UP, wo_rows(zl), wo_rows(zl), hdid(jnp.minimum(zl + 1, 3), y), zl < 3)
        send(WO_DN, wo_rows(zl), wo_rows(zl), hdid(jnp.maximum(zl - 1, 0), y), zl > 0)

    def wo_step(d):
        up, dn = zl >= d, zl + d <= 3
        recv(WO_UP + d - 1, wo_rows(zl - d), dpid(mate), up)
        if d < 3:
            send(WO_UP + d, wo_rows(zl - d), wo_rows(zl - d), hdid(jnp.minimum(zl + 1, 3), y), up & (zl < 3))
        send(WO_UPP + d - 1, wo_rows(zl - d), wo_rows(zl - d), dpid(mate), up)
        recv(WO_DN + d - 1, wo_rows(zl + d), dpid(mate), dn)
        if d < 3:
            send(WO_DN + d, wo_rows(zl + d), wo_rows(zl + d), hdid(jnp.maximum(zl - 1, 0), y), dn & (zl > 0))
        send(WO_DNP + d - 1, wo_rows(zl + d), wo_rows(zl + d), dpid(mate), dn)

    def wo_finish():
        for d in range(1, 4):
            recv(WO_UPP + d - 1, wo_mate_rows(zl - d), dpid(mate), zl >= d)
            recv(WO_DNP + d - 1, wo_mate_rows(zl + d), dpid(mate), zl + d <= 3)

    weights.near()
    weights.cross()
    own_copy.wait()
    wo_start()
    weights.near_rest()

    k_half = D // 2
    k_own = pl.multiple_of(zh * k_half, k_half)
    k_far = pl.multiple_of((1 - zh) * k_half, k_half)
    for n in range(0, 640, 128):
        u_buf[:, n : n + 128] = dot(nrm[:, pl.ds(k_own, k_half)], w_buf[pl.ds(k_own, k_half), n : n + 128])

    weights.far()

    for j in range(DP):
        rows = jnp.concatenate([wdt_all[j], jnp.zeros((120, 128), F32)], axis=0).T
        wdt_mat[ROWS * j : ROWS * j + ROWS, :] = rows[0:ROWS, :].astype(BF16)
    dt_cols = dot(nrm[16:EXT, :], wdt_mat[...])
    dt_rows = dt_cols.T[0:8, :].astype(BF16).astype(F32)
    sub = lax.broadcasted_iota(jnp.int32, (8, TOK), 0)
    lane = lax.broadcasted_iota(jnp.int32, (8, TOK), 1)

    def by_head(ref, s):
        return jnp.where(s == 0, ref[0], jnp.where(s == 1, ref[1], ref[2]))

    pre = dt_rows + by_head(dtb_ref, sub)
    step_rows = jnp.maximum(pre, 0.0) + jnp.log1p(jnp.exp(-jnp.abs(pre)))
    rate_rows = -step_rows * jnp.exp(by_head(alog_ref, sub))
    prefix = lane_cumsum(rate_rows)
    id8 = jnp.broadcast_to(id_row, (8, TOK))
    at_end = run_end(prefix, id8)
    first_end = at_end[:, 0:1]
    total = prefix[:, TOK - 1 : TOK]
    info_tx[0:8, :] = jnp.broadcast_to(first_end, (8, 128))
    info_tx[8:16, :] = jnp.broadcast_to(total, (8, 128))
    for j in range(4):
        send(INFO_UP + j, info_tx, info_rx.at[j], dpid(lax.rem(dp + j + 1, DP)), dp + j + 1 < DP)
        send(INFO_DN + j, info_tx, info_rx.at[4 + j], dpid(lax.rem(dp - j - 1 + DP, DP)), dp >= j + 1)

    to_end = jnp.exp(at_end - prefix) * step_rows
    cols[...] = jnp.concatenate([prefix, jnp.zeros((120, TOK), F32)], axis=0).T

    for n in range(0, 640, 128):
        u_buf[:, n : n + 128] += dot(nrm[:, pl.ds(k_far, k_half)], w_buf[pl.ds(k_far, k_half), n : n + 128])

    for r in range(0, EXT, 176):
        u_buf[r : r + 176, :] = u_buf[r : r + 176, :].astype(BF16).astype(F32)

    for q in range(4):
        r = 128 * q
        now = idc[16 + r : 144 + r, :]
        same = [jnp.where(idc[13 + k + r : 141 + k + r, :] == now, 1.0, 0.0) for k in range(3)]

        def conv(col, tap):
            acc = taps[3:4, tap : tap + 128] * u_buf[16 + r : 144 + r, col : col + 128]
            for k in range(3):
                acc = acc + same[k] * (
                    taps[k : k + 1, tap : tap + 128] * u_buf[13 + k + r : 141 + k + r, col : col + 128]
                )
            return (acc * jax.nn.sigmoid(acc)).astype(BF16)

        x0 = conv(0, 0)
        x1 = conv(128, 128)
        x_b[r : r + 128, 0:128] = x0
        x_b[r : r + 128, 128:256] = x1
        x_t[0:128, r : r + 128] = x0.astype(F32).T
        x_t[128:192, r : r + 128] = x1.astype(F32).T[0:64, :]
        b_b[r : r + 128, :] = conv(384, 256)
        c_b[r : r + 128, :] = conv(512, 384)

    last_id = id_row[:, TOK - 1 : TOK]
    is_last = id8 == jnp.broadcast_to(last_id, (8, TOK))

    def weighted_x(weight):
        return jnp.concatenate(
            [x_t[64 * h : 64 * h + 64, :] * weight[h : h + 1, :] for h in range(HEADS)], axis=0
        ).astype(BF16)

    l_tx[...] = dot(weighted_x(jnp.where(is_last, to_end, 0.0)), b_b[...]).astype(BF16)
    for j in range(4):
        send(STATE + j, l_tx, l_rx.at[j], dpid(lax.rem(dp + j + 1, DP)), dp + j + 1 < DP)

    def first_id(k):
        return ids_ref[jnp.clip(k, 0, DP - 1)][0:1, 0:1]

    def final_id(k):
        return ids_ref[jnp.clip(k, 0, DP - 1)][3:4, 127:128]

    one = jnp.zeros((1, 1), jnp.int32)
    for j in range(4):
        recv(INFO_DN + j, info_rx.at[4 + j], dpid(mate), dp + j + 1 < DP)
    after = jnp.zeros((8, 128), F32)
    for j in range(4):
        goes_on = (first_id(dp + j + 1) == final_id(dp)) & (one + dp + j + 1 < DP)
        after = after + jnp.where(goes_on, info_rx[4 + j, 0:8, :], 0.0)
    carry_on = jnp.broadcast_to(jnp.exp(after)[:, 0:1], (8, TOK))
    xw_end = weighted_x(to_end * jnp.where(is_last, carry_on, 1.0))
    for g in range(PROMPTS):
        mine = jnp.where(idc[16:EXT, :] == float(g), 1.0, 0.0).astype(BF16)
        b_all[:, 128 * g : 128 * g + 128] = b_b[...] * mine
    for g in range(PROMPTS):
        loc[g] = dot(xw_end, b_all[:, 128 * g : 128 * g + 128]).astype(BF16)
    mate_half = pl.multiple_of((1 - c) * 96, 96)
    send(TAB0, loc.at[:, pl.ds(mate_half, 96), :], tab0, dpid(mate))

    scol = lax.broadcasted_iota(jnp.int32, (128, TOK), 1)
    srow = lax.broadcasted_iota(jnp.int32, (128, TOK), 0)
    for q in range(4):
        r = 128 * q
        w = r + 128
        scores = dot_t(c_b[r:w, :], b_b[0:w, :])
        ok = (jnp.broadcast_to(idc[16 + r : 16 + w, 0:1], (128, w)) == jnp.broadcast_to(id_row[:, 0:w], (128, w))) & (
            scol[:, 0:w] <= srow[:, 0:w] + r
        )
        scores = jnp.where(ok, scores, 0.0)
        parts = []
        for h in range(HEADS):
            gap = jnp.broadcast_to(cols[r:w, h : h + 1], (128, w)) - prefix[h : h + 1, 0:w]
            mix = (scores * (jnp.exp(jnp.minimum(gap, 0.0)) * step_rows[h : h + 1, 0:w])).astype(BF16)
            col = 0 if h < 2 else 128
            parts.append(dot(mix, x_b[0:w, col : col + 128]))
        low = lax.broadcasted_iota(jnp.int32, (128, 128), 1) < 64
        smask[r:w, 0:128] = jnp.where(low, parts[0], parts[1])
        smask[r:w, 128:256] = parts[2]

    my_half = pl.multiple_of(c * 96, 96)
    recv(TAB0, tab0, dpid(mate))
    for g in range(PROMPTS):
        tabs[g] = (loc[g, pl.ds(my_half, 96), :].astype(F32) + tab0[g].astype(F32)).astype(BF16)
    send(TABZ, tabs.at[pl.ds(4 - 2 * zh, 2)], tabz, dpid(across))

    wo_step(1)

    for j in range(4):
        recv(INFO_UP + j, info_rx.at[j], dpid(mate), dp >= j + 1)
        recv(STATE + j, l_rx.at[j], dpid(mate), dp >= j + 1)
    state = l_rx[3].astype(F32)
    for j in (2, 1, 0):
        joined = (final_id(dp - j - 1) == final_id(dp - j - 2)) & (one + dp - j - 2 >= 0)
        gain_j = jnp.where(joined, jnp.exp(info_rx[j, 8:16, :]), 0.0)
        rows = jnp.concatenate(
            [jnp.broadcast_to(gain_j[h : h + 1, :], (64, 128)) for h in range(HEADS)], axis=0
        )
        state = l_rx[j].astype(F32) + rows * state
    s_in[0:FEAT, :] = state.astype(BF16)
    s_in[FEAT:256, :] = jnp.zeros((64, NSTATE), BF16)

    before_id = jnp.where(one + dp > 0, final_id(dp - 1), -1).astype(F32)
    lane1 = lax.broadcasted_iota(jnp.int32, (128, 128), 1)
    low = lane1 < 64
    skip0 = jnp.where(low, skip_ref[0], skip_ref[1])
    skip1 = jnp.where(low, skip_ref[2], 0.0)
    og0 = og_ref[:, 0:128]
    og1 = jnp.concatenate([og_ref[:, 128:192], jnp.zeros((1, 64), F32)], axis=1)
    for q in range(4):
        r = 128 * q
        w = r + 128
        inter = dot_t(c_b[r:w, :], s_in[...])
        enters = jnp.where(idc[16 + r : 16 + w, :] == before_id, 1.0, 0.0)
        decay = jnp.exp(cols[r:w, :])
        e0 = jnp.broadcast_to(decay[:, 0:1], (128, 128))
        e1 = jnp.broadcast_to(decay[:, 1:2], (128, 128))
        e2 = jnp.broadcast_to(decay[:, 2:3], (128, 128))
        y0 = smask[r:w, 0:128] + enters * jnp.where(low, e0, e1) * inter[:, 0:128]
        y1 = smask[r:w, 128:256] + enters * e2 * inter[:, 128:256]
        y0 = y0 + skip0 * x_b[r:w, 0:128].astype(F32)
        y1 = y1 + skip1 * x_b[r:w, 128:256].astype(F32)
        z0 = u_buf[16 + r : 16 + w, 256:384]
        z1 = jnp.where(low, pltpu.roll(u_buf[16 + r : 16 + w, 128:256], 64, 1), 0.0)
        g0 = y0 * (z0 * jax.nn.sigmoid(z0))
        g1 = y1 * (z1 * jax.nn.sigmoid(z1))
        sq = jnp.sum(g0 * g0 + g1 * g1, axis=1, keepdims=True)
        hi = sq.astype(BF16).astype(F32)
        g_send[r:w, 0:128] = (g0 * og0).astype(BF16)
        g_send[r:w, 128:256] = jnp.where(
            low, g1 * og1, jnp.where(lane1 == 64, hi, jnp.where(lane1 == 65, sq - hi, 0.0))
        ).astype(BF16)
    for k in range(1, 4):
        zt = lax.rem(zl + k, 4)
        send(
            A2A + k - 1, g_send.at[pl.ds(pl.multiple_of(zt * 128, 128), 128), :], a_rx.at[zl],
            hdid(zt, y),
        )
    a_rx[zl] = g_send[pl.ds(pl.multiple_of(zl * 128, 128), 128), :]

    wo_step(2)
    wo_step(3)

    recv(TABZ, tabz, dpid(across))
    tabm[...] = tabs[pl.ds(4 * zh, 4)]
    mid = 2 - 2 * zh
    tabm[pl.ds(mid, 2)] = (tabs[pl.ds(4 * zh + mid, 2)].astype(F32) + tabz[...].astype(F32)).astype(BF16)
    for k in range(1, 4):
        xt = lax.rem(x + k, 4)
        send(TABX + k - 1, tabm.at[xt], tabx.at[k - 1], dpid(dev(zh, xt, c)))

    wo_finish()

    for k in range(1, 4):
        zs = lax.rem(zl + 4 - k, 4)
        recv(A2A + k - 1, a_rx.at[zs], hdid(zs, y))
    sq = jnp.zeros((128, 1), F32)
    picked = (lane1 == 64) | (lane1 == 65)
    for z_ in range(4):
        sq = sq + jnp.sum(jnp.where(picked, a_rx[z_, :, 128:256].astype(F32), 0.0), axis=1, keepdims=True)
    hi = sq.astype(BF16).astype(F32)
    tail = jnp.where(lane1 == 0, hi, jnp.where(lane1 == 1, sq - hi, 0.0))
    own_acc[:, D : D + 128] = tail
    part[:, :, D : D + 128] = tail.astype(BF16).reshape(4, 32, 128)
    for n in range(0, D, 256):
        acc = dot(a_rx[0, :, 0:FEAT], wo[0, :, n : n + 256])
        for z_ in range(1, 4):
            acc = acc + dot(a_rx[z_, :, 0:FEAT], wo[z_, :, n : n + 256])
        own_acc[:, n : n + 256] = acc
        part[:, :, n : n + 256] = acc.astype(BF16).reshape(4, 32, 256)
    for k in range(1, 4):
        yt = lax.rem(y + k, 4)
        send(RSY + k - 1, part.at[yt], rs_rx.at[k - 1], hdid(zl, yt))

    for k in range(1, 4):
        recv(TABX + k - 1, tabx.at[k - 1], dpid(mate))
    done = tabm[x].astype(F32)
    for k in range(3):
        done = done + tabx[k].astype(F32)
    fin[dp // 2, pl.ds(my_half, 96), :] = done.astype(BF16)

    def f_rows(owner):
        return fin.at[owner // 2, pl.ds(pl.multiple_of(lax.rem(owner, 2) * 96, 96), 96), :]

    finals = Gather([(F_IDS, f_rows)])
    finals.own()

    for k in range(1, 4):
        recv(RSY + k - 1, rs_rx.at[k - 1], hdid(zl, lax.rem(y + 4 - k, 4)))
    y_rows = pl.ds(pl.multiple_of(y * 32, 32), 32)
    sq = own_acc[y_rows, D : D + 128]
    for k in range(3):
        sq = sq + rs_rx[k, :, D : D + 128].astype(F32)
    scale = lax.rsqrt(jnp.sum(sq, axis=1, keepdims=True) / (FEAT * HD) + EPSILON)
    acc = own_acc[y_rows, 0:D]
    for k in range(3):
        acc = acc + rs_rx[k, :, 0:D].astype(F32)
    resid = hid_ref[pl.ds(pl.multiple_of(hd * 32, 32), 32), :].astype(F32)
    out_ref[...] = (resid + scale * acc).astype(BF16)

    finals.near()
    finals.cross()
    finals.near_rest()
    finals.far()
    for r in range(4):
        st_ref[r] = fin[req_ref[r]].astype(F32)

    for m, src, dst, to, cond in pending:
        if cond is None:
            msg(m, src, dst, to).wait_send()
        else:
            @pl.when(cond)
            def _():
                msg(m, src, dst, to).wait_send()


def on_device(
    hidden, token_prompt, request_prompt, in_gain, w_zx, w_bc, w_dt, dt_bias, a_log, conv_x,
    conv_bc, skip_gain, out_gain, w_out,
):
    vmem = pl.BlockSpec(memory_space=pltpu.VMEM)
    smem = pl.BlockSpec(memory_space=pltpu.SMEM)
    layer_out, states = pl.pallas_call(
        body,
        out_shape=(
            jax.ShapeDtypeStruct((TOK // HD, D), BF16),
            jax.ShapeDtypeStruct((4, FEAT, NSTATE), F32),
        ),
        in_specs=[vmem, smem, smem, smem, smem] + [vmem] * 9,
        out_specs=(vmem, vmem),
        scratch_shapes=[
            pltpu.VMEM((D, 640), BF16),
            pltpu.VMEM((ROWS, 640), F32),
            pltpu.VMEM((DP, 8, 128), F32),
            pltpu.VMEM((D, 128), BF16),
            pltpu.VMEM((16, D), BF16),
            pltpu.VMEM((EXT, D), BF16),
            pltpu.VMEM((EXT, 128), F32),
            pltpu.VMEM((EXT, 640), F32),
            pltpu.VMEM((8, 512), F32),
            pltpu.VMEM((FEAT, TOK), F32),
            pltpu.VMEM((TOK, 256), BF16),
            pltpu.VMEM((TOK, 128), BF16),
            pltpu.VMEM((TOK, 128), BF16),
            pltpu.VMEM((TOK, 128 * PROMPTS), BF16),
            pltpu.VMEM((16, 128), F32),
            pltpu.VMEM((8, 16, 128), F32),
            pltpu.VMEM((FEAT, NSTATE), BF16),
            pltpu.VMEM((4, FEAT, NSTATE), BF16),
            pltpu.VMEM((256, NSTATE), BF16),
            pltpu.VMEM((TOK, 128), F32),
            pltpu.VMEM((TOK, 256), F32),
            pltpu.VMEM((PROMPTS, FEAT, NSTATE), BF16),
            pltpu.VMEM((PROMPTS, 96, NSTATE), BF16),
            pltpu.VMEM((PROMPTS, 96, NSTATE), BF16),
            pltpu.VMEM((2, 96, NSTATE), BF16),
            pltpu.VMEM((4, 96, NSTATE), BF16),
            pltpu.VMEM((3, 96, NSTATE), BF16),
            pltpu.VMEM((PROMPTS, FEAT, NSTATE), BF16),
            pltpu.VMEM((TOK, 256), BF16),
            pltpu.VMEM((4, 128, 256), BF16),
            pltpu.VMEM((4, FEAT, D), BF16),
            pltpu.VMEM((4, 32, OUTW), BF16),
            pltpu.VMEM((128, OUTW), F32),
            pltpu.VMEM((3, 32, OUTW), BF16),
            pltpu.SemaphoreType.DMA((N_MSG,)),
            pltpu.SemaphoreType.DMA((N_MSG,)),
            pltpu.SemaphoreType.DMA,
        ],
        compiler_params=pltpu.CompilerParams(
            collective_id=0, has_side_effects=True, vmem_limit_bytes=60 * 2**20
        ),
        name="layer",
    )(
        token_prompt.reshape(DP, 4, 128), request_prompt, dt_bias, a_log, skip_gain, hidden,
        in_gain.reshape(1, D), w_zx, w_bc, w_dt, conv_x, conv_bc, out_gain.reshape(1, FEAT), w_out,
    )
    return layer_out, states.reshape(4, HEADS, 64, NSTATE)


def solution(mesh):
    in_specs = (
        P("dp", None), P(), P("dp"), P(), P("dp", None, "head"), P("dp", None), P("dp", "head"),
        P("head"), P("head"), P(None, "head"), P(), P("head"), P("head"), P("head", None),
    )
    out_specs = (P(("dp", "head"), None), P("dp", "head", None, None))
    return jax.shard_map(on_device, mesh=mesh, in_specs=in_specs, out_specs=out_specs, check_vma=False)
```

time: 483 us -> 93.3 us (0.19)
  the two profiles are of different devices: /device:TPU:2 before, /device:TPU:1 now
where the time goes in v1:
time: 93.3 us; the launch traced here: 93 us
  Pallas kernels  86.4 us (93%)
  local copies, waits for them, and re-layouts  6 us (6%)
    pallas_call x1, Pallas kernels, on_device(): pl.pallas_call(body, out_shape=(jax.ShapeDtypeStruct((TOK // HD, D), BF16...  86.4 us
    unnamed x3, local copies, waits for them, and re-layouts  4.7 us

profile of v1, /device:TPU:1, one launch (start us, length us, event | category | flops | bytes accessed | tf_op | source)
XLA Modules:
  0.0 93.0 jit_solution(4306995546979446843)
XLA Ops:
  0.6 1.3 %reshape.17.gain_ref = f32[1,1536]{1,0:T(1,128)} reshape(f32[1536]{0:T(1024)} %param.17) | data formatting | bytes 12288 | tf_op jit(solution)/shard_map/reshape | solution.py:619
  1.9 1.4 %copy.16.wdt_ref = f32[96,3]{1,0:T(8,128)} copy(f32[96,3]{0,1:T(4,128)} %param.20) | data formatting | bytes 2304 | tf_op args[6]
  3.3 86.4 %layer.1 = (bf16[32,1536]{1,0:T(8,128)(2,1)}, f32[4,192,128]{2,1,0:T(8,128)}) custom-call(s32[16,4,128]{2,1,0:T(4,128)} %bitcast.4, s32[4]{0:T(128)} %req_ref.1, f32[3]{0:T(128)} %dtb_ref.1, f32[3]{0:T(128)} %alog_ref.1, f32[3]{0:T(128)} %skip_ref.1, bf16[512,1536]{1,0:T(8,128)(2,1)} %hid_ref.1, f32[1,1536]{1,0:T(1,128)} %reshape.17.gain_ref, ...), custom_call_target="tpu_custom_call" | custom-call | tf_op jit(solution)/shard_map/layer/pallas_call | solution.py:566
  89.7 1.5 %copy.19 = bf16[32,1536]{1,0:T(8,128)(2,1)} copy(bf16[32,1536]{1,0:T(8,128)(2,1)} %get-tuple-element.8) | data formatting | bytes 196608
  91.3 1.8 %copy.20 = f32[4,3,64,128]{3,2,1,0:T(8,128)} copy(f32[4,3,64,128]{3,2,1,0:T(8,128)} %bitcast.3) | data formatting | bytes 786432

commit v2 on v1

--- a/solution.py
+++ b/solution.py
@@ -29,16 +29,14 @@
 INFO_UP = 46
 INFO_DN = 50
 STATE = 54
-WO_UP = 58
-WO_DN = 64
-WO_UPP = 70
-WO_DNP = 76
-TAB0 = 82
-TABZ = 83
-TABX = 84
-A2A = 87
-RSY = 90
-N_MSG = 93
+WO = 58
+WO_MATE = 61
+TAB0 = 64
+TABZ = 65
+TABX = 66
+A2A = 69
+RSZ = 72
+N_MSG = 75
 
 
 def dot(a, b):
@@ -68,6 +66,20 @@
         v = jnp.where(same, pltpu.roll(v, width - step, 1), v)
         step *= 2
     return v
+
+
+SCOPE = []
+
+
+def phase(name):
+    if SCOPE:
+        SCOPE.pop().__exit__(None, None, None)
+    if name and TRACE:
+        SCOPE.append(jax.named_scope(name))
+        SCOPE[-1].__enter__()
+
+
+TRACE = False
 
 
 def body(
@@ -179,6 +191,7 @@
             self.recv(13, dev(o, x - sgn, 1 - c))
             self.recv(14, dev(o, x + 2, 1 - c))
 
+    phase("entry")
     barrier = pltpu.get_barrier_semaphore()
     for k in range(1, DP):
         pl.semaphore_signal(
@@ -200,14 +213,8 @@
     wst[:, 384:640] = wbc_ref[...]
     own_rows = pl.multiple_of(dp * ROWS, ROWS)
     w_buf[pl.ds(own_rows, ROWS), :] = wst[...].astype(BF16)
-    wdt_pad = jnp.concatenate(
-        [
-            jnp.concatenate([wdt_ref[...], jnp.zeros((ROWS, 125), F32)], axis=1),
-            jnp.zeros((32, 128), F32),
-        ],
-        axis=0,
-    )
-    wdt_all[dp] = wdt_pad.T[0:8, :]
+    wdt_all[dp] = jnp.zeros((8, 128), F32)
+    wdt_all[dp, 0:HEADS, 0:ROWS] = wdt_ref[...]
 
     def w_rows(owner):
         return w_buf.at[pl.ds(pl.multiple_of(owner * ROWS, ROWS), ROWS), :]
@@ -216,7 +223,7 @@
         return wdt_all.at[owner]
 
     weights = Gather([(W_IDS, w_rows), (T_IDS, t_rows)])
-    own_copy = pltpu.make_async_copy(wout_ref, wo.at[zl], local_sem)
+    own_copy = pltpu.make_async_copy(wout_ref, wo.at[y], local_sem)
     own_copy.start()
 
     @pl.when(dp == 0)
@@ -237,6 +244,14 @@
 
     weights.own()
     send(HALO, hid_ref.at[pl.ds(TOK - 16, 16), :], halo, dpid(lax.rem(dp + 1, DP)), dp < DP - 1)
+
+    phase("ids")
+    def wo_rows(y_, c_):
+        return wo.at[lax.rem(y_ + 4, 4), pl.ds(pl.multiple_of(c_ * 96, 96), 96), :]
+
+    own_copy.wait()
+    for k in (1, 3, 2):
+        send(WO + k - 1, wo_rows(y, c), wo_rows(y, c), hdid(zl, lax.rem(y + k, 4)))
 
     own_ids = ids_ref[dp].astype(F32)
     prev_ids = ids_ref[jnp.maximum(dp - 1, 0)].astype(F32)
@@ -252,7 +267,8 @@
     taps[0:4, 128:192] = cx_ref[:, 128:192]
     taps[0:4, 256:512] = cbc_ref[...]
 
-    gain = gain_ref[...]
+    phase("norm")
+    gain = gain_ref[...].reshape(1, D)
 
     def norm_rows(rows):
         h = rows.astype(F32)
@@ -265,51 +281,28 @@
         return carry
 
     lax.fori_loop(0, TOK // 32, norm_step, 0)
+    phase("halo_wait")
     recv(HALO, halo, dpid(mate), dp > 0)
     nrm[0:16, :] = norm_rows(halo[...])
 
-    half = pl.multiple_of(c * 96, 96)
-
-    def wo_rows(z_):
-        return wo.at[jnp.clip(z_, 0, 3), pl.ds(half, 96), :]
-
-    def wo_mate_rows(z_):
-        return wo.at[jnp.clip(z_, 0, 3), pl.ds(pl.multiple_of((1 - c) * 96, 96), 96), :]
-
-    def wo_start():
-        send(WO_UP, wo_rows(zl), wo_rows(zl), hdid(jnp.minimum(zl + 1, 3), y), zl < 3)
-        send(WO_DN, wo_rows(zl), wo_rows(zl), hdid(jnp.maximum(zl - 1, 0), y), zl > 0)
-
-    def wo_step(d):
-        up, dn = zl >= d, zl + d <= 3
-        recv(WO_UP + d - 1, wo_rows(zl - d), dpid(mate), up)
-        if d < 3:
-            send(WO_UP + d, wo_rows(zl - d), wo_rows(zl - d), hdid(jnp.minimum(zl + 1, 3), y), up & (zl < 3))
-        send(WO_UPP + d - 1, wo_rows(zl - d), wo_rows(zl - d), dpid(mate), up)
-        recv(WO_DN + d - 1, wo_rows(zl + d), dpid(mate), dn)
-        if d < 3:
-            send(WO_DN + d, wo_rows(zl + d), wo_rows(zl + d), hdid(jnp.maximum(zl - 1, 0), y), dn & (zl > 0))
-        send(WO_DNP + d - 1, wo_rows(zl + d), wo_rows(zl + d), dpid(mate), dn)
-
-    def wo_finish():
-        for d in range(1, 4):
-            recv(WO_UPP + d - 1, wo_mate_rows(zl - d), dpid(mate), zl >= d)
-            recv(WO_DNP + d - 1, wo_mate_rows(zl + d), dpid(mate), zl + d <= 3)
-
+    phase("w_near")
     weights.near()
+    phase("w_cross")
     weights.cross()
-    own_copy.wait()
-    wo_start()
+    phase("w_near_rest")
     weights.near_rest()
 
+    phase("mm1")
     k_half = D // 2
     k_own = pl.multiple_of(zh * k_half, k_half)
     k_far = pl.multiple_of((1 - zh) * k_half, k_half)
     for n in range(0, 640, 128):
         u_buf[:, n : n + 128] = dot(nrm[:, pl.ds(k_own, k_half)], w_buf[pl.ds(k_own, k_half), n : n + 128])
 
+    phase("w_far")
     weights.far()
 
+    phase("dt")
     for j in range(DP):
         rows = jnp.concatenate([wdt_all[j], jnp.zeros((120, 128), F32)], axis=0).T
         wdt_mat[ROWS * j : ROWS * j + ROWS, :] = rows[0:ROWS, :].astype(BF16)
@@ -338,9 +331,11 @@
     to_end = jnp.exp(at_end - prefix) * step_rows
     cols[...] = jnp.concatenate([prefix, jnp.zeros((120, TOK), F32)], axis=0).T
 
+    phase("mm2")
     for n in range(0, 640, 128):
         u_buf[:, n : n + 128] += dot(nrm[:, pl.ds(k_far, k_half)], w_buf[pl.ds(k_far, k_half), n : n + 128])
 
+    phase("conv")
     for r in range(0, EXT, 176):
         u_buf[r : r + 176, :] = u_buf[r : r + 176, :].astype(BF16).astype(F32)
 
@@ -366,6 +361,7 @@
         b_b[r : r + 128, :] = conv(384, 256)
         c_b[r : r + 128, :] = conv(512, 384)
 
+    phase("lstate")
     last_id = id_row[:, TOK - 1 : TOK]
     is_last = id8 == jnp.broadcast_to(last_id, (8, TOK))
 
@@ -378,6 +374,7 @@
     for j in range(4):
         send(STATE + j, l_tx, l_rx.at[j], dpid(lax.rem(dp + j + 1, DP)), dp + j + 1 < DP)
 
+    phase("table_loc")
     def first_id(k):
         return ids_ref[jnp.clip(k, 0, DP - 1)][0:1, 0:1]
 
@@ -401,6 +398,11 @@
     mate_half = pl.multiple_of((1 - c) * 96, 96)
     send(TAB0, loc.at[:, pl.ds(mate_half, 96), :], tab0, dpid(mate))
 
+    phase("wo_mate")
+    for k in (1, 3, 2):
+        recv(WO + k - 1, wo_rows(y - k, c), dpid(mate))
+        send(WO_MATE + k - 1, wo_rows(y - k, c), wo_rows(y - k, c), dpid(mate))
+    phase("scores")
     scol = lax.broadcasted_iota(jnp.int32, (128, TOK), 1)
     srow = lax.broadcasted_iota(jnp.int32, (128, TOK), 0)
     for q in range(4):
@@ -421,14 +423,14 @@
         smask[r:w, 0:128] = jnp.where(low, parts[0], parts[1])
         smask[r:w, 128:256] = parts[2]
 
+    phase("tab0_wait")
     my_half = pl.multiple_of(c * 96, 96)
     recv(TAB0, tab0, dpid(mate))
     for g in range(PROMPTS):
         tabs[g] = (loc[g, pl.ds(my_half, 96), :].astype(F32) + tab0[g].astype(F32)).astype(BF16)
     send(TABZ, tabs.at[pl.ds(4 - 2 * zh, 2)], tabz, dpid(across))
 
-    wo_step(1)
-
+    phase("state_wait")
     for j in range(4):
         recv(INFO_UP + j, info_rx.at[j], dpid(mate), dp >= j + 1)
         recv(STATE + j, l_rx.at[j], dpid(mate), dp >= j + 1)
@@ -443,6 +445,7 @@
     s_in[0:FEAT, :] = state.astype(BF16)
     s_in[FEAT:256, :] = jnp.zeros((64, NSTATE), BF16)
 
+    phase("yinter")
     before_id = jnp.where(one + dp > 0, final_id(dp - 1), -1).astype(F32)
     lane1 = lax.broadcasted_iota(jnp.int32, (128, 128), 1)
     low = lane1 < 64
@@ -469,21 +472,16 @@
         g1 = y1 * (z1 * jax.nn.sigmoid(z1))
         sq = jnp.sum(g0 * g0 + g1 * g1, axis=1, keepdims=True)
         hi = sq.astype(BF16).astype(F32)
-        g_send[r:w, 0:128] = (g0 * og0).astype(BF16)
-        g_send[r:w, 128:256] = jnp.where(
+        g_send[q, :, :, 0:128] = (g0 * og0).astype(BF16).reshape(4, 32, 128)
+        g_send[q, :, :, 128:256] = jnp.where(
             low, g1 * og1, jnp.where(lane1 == 64, hi, jnp.where(lane1 == 65, sq - hi, 0.0))
-        ).astype(BF16)
-    for k in range(1, 4):
-        zt = lax.rem(zl + k, 4)
-        send(
-            A2A + k - 1, g_send.at[pl.ds(pl.multiple_of(zt * 128, 128), 128), :], a_rx.at[zl],
-            hdid(zt, y),
-        )
-    a_rx[zl] = g_send[pl.ds(pl.multiple_of(zl * 128, 128), 128), :]
-
-    wo_step(2)
-    wo_step(3)
-
+        ).astype(BF16).reshape(4, 32, 128)
+    for k in (2, 1, 3):
+        yt = lax.rem(y + k, 4)
+        send(A2A + k - 1, g_send.at[:, yt], a_rx.at[y], hdid(zl, yt))
+    a_rx[y] = g_send[:, y]
+
+    phase("tabz_wait")
     recv(TABZ, tabz, dpid(across))
     tabm[...] = tabs[pl.ds(4 * zh, 4)]
     mid = 2 - 2 * zh
@@ -492,29 +490,35 @@
         xt = lax.rem(x + k, 4)
         send(TABX + k - 1, tabm.at[xt], tabx.at[k - 1], dpid(dev(zh, xt, c)))
 
-    wo_finish()
-
+    phase("wo_finish")
+    for k in (1, 3, 2):
+        recv(WO_MATE + k - 1, wo_rows(y - k, 1 - c), dpid(mate))
+
+    phase("a2a_wait")
     for k in range(1, 4):
-        zs = lax.rem(zl + 4 - k, 4)
-        recv(A2A + k - 1, a_rx.at[zs], hdid(zs, y))
+        ys = lax.rem(y + 4 - k, 4)
+        recv(A2A + k - 1, a_rx.at[ys], hdid(zl, ys))
+    phase("outproj")
     sq = jnp.zeros((128, 1), F32)
     picked = (lane1 == 64) | (lane1 == 65)
-    for z_ in range(4):
-        sq = sq + jnp.sum(jnp.where(picked, a_rx[z_, :, 128:256].astype(F32), 0.0), axis=1, keepdims=True)
+    for y_ in range(4):
+        tails = a_rx[y_, :, :, 128:256].reshape(128, 128).astype(F32)
+        sq = sq + jnp.sum(jnp.where(picked, tails, 0.0), axis=1, keepdims=True)
     hi = sq.astype(BF16).astype(F32)
     tail = jnp.where(lane1 == 0, hi, jnp.where(lane1 == 1, sq - hi, 0.0))
     own_acc[:, D : D + 128] = tail
     part[:, :, D : D + 128] = tail.astype(BF16).reshape(4, 32, 128)
     for n in range(0, D, 256):
-        acc = dot(a_rx[0, :, 0:FEAT], wo[0, :, n : n + 256])
-        for z_ in range(1, 4):
-            acc = acc + dot(a_rx[z_, :, 0:FEAT], wo[z_, :, n : n + 256])
+        acc = jnp.zeros((128, 256), F32)
+        for y_ in range(4):
+            acc = acc + dot(a_rx[y_, :, :, 0:FEAT].reshape(128, FEAT), wo[y_, :, n : n + 256])
         own_acc[:, n : n + 256] = acc
         part[:, :, n : n + 256] = acc.astype(BF16).reshape(4, 32, 256)
-    for k in range(1, 4):
-        yt = lax.rem(y + k, 4)
-        send(RSY + k - 1, part.at[yt], rs_rx.at[k - 1], hdid(zl, yt))
-
+    for k in (2, 1, 3):
+        zt = lax.rem(zl + k, 4)
+        send(RSZ + k - 1, part.at[zt], rs_rx.at[k - 1], hdid(zt, y))
+
+    phase("tabx_wait")
     for k in range(1, 4):
         recv(TABX + k - 1, tabx.at[k - 1], dpid(mate))
     done = tabm[x].astype(F32)
@@ -525,29 +529,38 @@
     def f_rows(owner):
         return fin.at[owner // 2, pl.ds(pl.multiple_of(lax.rem(owner, 2) * 96, 96), 96), :]
 
+    phase("fin_own")
     finals = Gather([(F_IDS, f_rows)])
     finals.own()
 
+    phase("fin_near")
+    finals.near()
+    phase("fin_cross")
+    finals.cross()
+    phase("fin_nearrest")
+    finals.near_rest()
+    phase("fin_far")
+    finals.far()
+    phase("rsy_wait")
     for k in range(1, 4):
-        recv(RSY + k - 1, rs_rx.at[k - 1], hdid(zl, lax.rem(y + 4 - k, 4)))
-    y_rows = pl.ds(pl.multiple_of(y * 32, 32), 32)
-    sq = own_acc[y_rows, D : D + 128]
+        recv(RSZ + k - 1, rs_rx.at[k - 1], hdid(lax.rem(zl + 4 - k, 4), y))
+    phase("out")
+    z_rows = pl.ds(pl.multiple_of(zl * 32, 32), 32)
+    sq = own_acc[z_rows, D : D + 128]
     for k in range(3):
         sq = sq + rs_rx[k, :, D : D + 128].astype(F32)
     scale = lax.rsqrt(jnp.sum(sq, axis=1, keepdims=True) / (FEAT * HD) + EPSILON)
-    acc = own_acc[y_rows, 0:D]
+    acc = own_acc[z_rows, 0:D]
     for k in range(3):
         acc = acc + rs_rx[k, :, 0:D].astype(F32)
     resid = hid_ref[pl.ds(pl.multiple_of(hd * 32, 32), 32), :].astype(F32)
     out_ref[...] = (resid + scale * acc).astype(BF16)
 
-    finals.near()
-    finals.cross()
-    finals.near_rest()
-    finals.far()
+    phase("st_out")
     for r in range(4):
-        st_ref[r] = fin[req_ref[r]].astype(F32)
-
+        st_ref[r] = fin[req_ref[r]]
+
+    phase("drain")
     for m, src, dst, to, cond in pending:
         if cond is None:
             msg(m, src, dst, to).wait_send()
@@ -555,6 +568,12 @@
             @pl.when(cond)
             def _():
                 msg(m, src, dst, to).wait_send()
+    phase(None)
+
+
+def write_out(rows_ref, states_ref, out_ref, st_ref):
+    out_ref[...] = rows_ref[...]
+    st_ref[...] = states_ref[...].astype(F32)
 
 
 def on_device(
@@ -567,7 +586,7 @@
         body,
         out_shape=(
             jax.ShapeDtypeStruct((TOK // HD, D), BF16),
-            jax.ShapeDtypeStruct((4, FEAT, NSTATE), F32),
+            jax.ShapeDtypeStruct((4, FEAT, NSTATE), BF16),
         ),
         in_specs=[vmem, smem, smem, smem, smem] + [vmem] * 9,
         out_specs=(vmem, vmem),
@@ -600,8 +619,8 @@
             pltpu.VMEM((4, 96, NSTATE), BF16),
             pltpu.VMEM((3, 96, NSTATE), BF16),
             pltpu.VMEM((PROMPTS, FEAT, NSTATE), BF16),
-            pltpu.VMEM((TOK, 256), BF16),
-            pltpu.VMEM((4, 128, 256), BF16),
+            pltpu.VMEM((4, 4, 32, 256), BF16),
+            pltpu.VMEM((4, 4, 32, 256), BF16),
             pltpu.VMEM((4, FEAT, D), BF16),
             pltpu.VMEM((4, 32, OUTW), BF16),
             pltpu.VMEM((128, OUTW), F32),
@@ -616,8 +635,18 @@
         name="layer",
     )(
         token_prompt.reshape(DP, 4, 128), request_prompt, dt_bias, a_log, skip_gain, hidden,
-        in_gain.reshape(1, D), w_zx, w_bc, w_dt, conv_x, conv_bc, out_gain.reshape(1, FEAT), w_out,
+        in_gain, w_zx, w_bc, w_dt.T, conv_x, conv_bc, out_gain.reshape(1, FEAT), w_out,
     )
+    layer_out, states = pl.pallas_call(
+        write_out,
+        out_shape=(
+            jax.ShapeDtypeStruct((TOK // HD, D), BF16),
+            jax.ShapeDtypeStruct((4, FEAT, NSTATE), F32),
+        ),
+        in_specs=[vmem, vmem],
+        out_specs=(vmem, vmem),
+        name="write_out",
+    )(layer_out, states)
     return layer_out, states.reshape(4, HEADS, 64, NSTATE)
 
 

time: 93.3 us -> 73.9 us (0.79)
  Pallas kernels: 86.4 us -> 72.8 us
  local copies, waits for them, and re-layouts: 6 us -> 0 us
    pallas_call x1, Pallas kernels: 86.4 us -> 71 us  [on_device(): pl.pallas_call(body, out_shape=(jax.ShapeDtypeStruct((TOK // HD, D), BF16...]
    unnamed x3 -> x0, local copies, waits for them, and re-layouts: 4.7 us -> none
    pallas_call x0 -> x1, Pallas kernels: none -> 1.76 us  [on_device(): pl.pallas_call(write_out, out_shape=(jax.ShapeDtypeStruct((TOK // HD, D),...]
    reshape x1 -> x0, local copies, waits for them, and re-layouts: 1.3 us -> none  [on_device(): in_gain.reshape(1, D)]
where the time goes in v2:
time: 73.9 us; the launch traced here: 73.4 us
  Pallas kernels  72.8 us (99%)
    pallas_call x1, Pallas kernels, on_device(): pl.pallas_call(body, out_shape=(jax.ShapeDtypeStruct((TOK // HD, D), BF16...  71 us
    pallas_call x1, Pallas kernels, on_device(): pl.pallas_call(write_out, out_shape=(jax.ShapeDtypeStruct((TOK // HD, D),...  1.76 us

profile of v2, /device:TPU:1, one launch (start us, length us, event | category | flops | bytes accessed | tf_op | source)
XLA Modules:
  0.0 73.4 jit_solution(5009659327057369403)
XLA Ops:
  0.6 71.0 %layer.1 = (bf16[32,1536]{1,0:T(8,128)(2,1)}, bf16[4,192,128]{2,1,0:T(8,128)(2,1)}) custom-call(s32[16,4,128]{2,1,0:T(4,128)} %bitcast.4, s32[4]{0:T(128)} %req_ref.1, f32[3]{0:T(128)} %dtb_ref.1, f32[3]{0:T(128)} %alog_ref.1, f32[3]{0:T(128)} %skip_ref.1, bf16[512,1536]{1,0:T(8,128)(2,1)} %hid_ref.1, f32[1536]{0:T(1024)} %gain_ref.1, ...), custom_call_target="tpu_custom_call" | custom-call | tf_op jit(solution)/shard_map/layer/pallas_call | solution.py:585
  71.7 1.8 %write_out.1 = (bf16[32,1536]{1,0:T(8,128)(2,1)}, f32[4,192,128]{2,1,0:T(8,128)}) custom-call(bf16[32,1536]{1,0:T(8,128)(2,1)} %get-tuple-element.6.rows_ref, bf16[4,192,128]{2,1,0:T(8,128)(2,1)} %get-tuple-element.7.states_ref), custom_call_target="tpu_custom_call" | custom-call | tf_op jit(solution)/shard_map/write_out/pallas_call | solution.py:640

commit v3 on v2

--- a/solution.py
+++ b/solution.py
@@ -36,7 +36,9 @@
 TABX = 66
 A2A = 69
 RSZ = 72
-N_MSG = 75
+BCZ = 75
+BCY = 78
+N_MSG = 81
 
 
 def dot(a, b):
@@ -83,9 +85,10 @@
 
 
 def body(
-    ids_ref, req_ref, dtb_ref, alog_ref, skip_ref, hid_ref, gain_ref, wzx_ref, wbc_ref,
-    wdt_ref, cx_ref, cbc_ref, og_ref, wout_ref, out_ref, st_ref,
-    w_buf, wst, wdt_all, wdt_mat, halo, nrm, idc, u_buf, taps, x_t, x_b, b_b, c_b, b_all,
+    req_ref, dtb_ref, alog_ref, skip_ref, wzx_in, wbc_in, wdt_in, ids_in, hid_in, gain_in,
+    cx_in, cbc_in, og_in, wout_in, out_ref, st_ref,
+    wzx_ref, wbc_ref, wdt_ref, ids_ref, hid_ref, gain_ref, cx_ref, cbc_ref, og_ref,
+    w_buf, wst, bc_t, sm_t, small, wdt_mat, bc_parts, halo, nrm, idc, u_buf, taps, x_t, x_b, b_b, c_b, b_all,
     info_tx, info_rx, l_tx, l_rx, s_in, cols, smask, loc, tab0, tabs, tabz, tabm, tabx, fin,
     g_send, a_rx, wo, part, own_acc, rs_rx, send_sem, recv_sem, local_sem,
 ):
@@ -96,13 +99,10 @@
     c = dp % 2
     zl = hd // 4
     y = hd % 4
-    sgn = 1 - 2 * c
 
     def dev(z_, x_, c_):
         return z_ * 8 + lax.rem(x_ + 8, 4) * 2 + c_
 
-    ahead = dev(zh, x + sgn, c)
-    behind = dev(zh, x - sgn, c)
     across = dev(1 - zh, x, c)
     mate = dev(zh, x, 1 - c)
 
@@ -152,44 +152,35 @@
 
         def own(self):
             self.send(3, dp, across)
-            self.send(0, dp, ahead)
-            self.send(1, dp, behind)
+            self.send(2, dp, dev(zh, x + 2, c))
+            self.send(0, dp, dev(zh, x + 1, c))
+            self.send(1, dp, dev(zh, x - 1, c))
             self.send(7, dp, mate)
 
+        def cross(self):
+            o = 1 - zh
+            self.recv(3, dev(o, x, c))
+            self.send(6, dev(o, x, c), dev(zh, x + 2, c))
+            self.send(4, dev(o, x, c), dev(zh, x + 1, c))
+            self.send(5, dev(o, x, c), dev(zh, x - 1, c))
+            self.send(11, dev(o, x, c), mate)
+
         def near(self):
-            self.recv(0, dev(zh, x - sgn, c))
-            self.send(2, dev(zh, x - sgn, c), ahead)
-            self.send(8, dev(zh, x - sgn, c), mate)
-            self.recv(1, dev(zh, x + sgn, c))
-            self.send(9, dev(zh, x + sgn, c), mate)
-
-        def cross(self):
-            self.recv(3, dev(1 - zh, x, c))
-            self.send(4, dev(1 - zh, x, c), ahead)
-            self.send(5, dev(1 - zh, x, c), behind)
-            self.send(11, dev(1 - zh, x, c), mate)
+            for k, step in ((0, -1), (1, 1), (2, 2)):
+                self.recv(k, dev(zh, x + step, c))
+                self.send(8 + k, dev(zh, x + step, c), mate)
 
         def near_rest(self):
-            self.recv(2, dev(zh, x + 2, c))
-            self.send(10, dev(zh, x + 2, c), mate)
-            self.recv(7, dev(zh, x, 1 - c))
-            self.recv(8, dev(zh, x + sgn, 1 - c))
-            self.recv(9, dev(zh, x - sgn, 1 - c))
-            self.recv(10, dev(zh, x + 2, 1 - c))
+            for k, step in ((7, 0), (8, -1), (9, 1), (10, 2)):
+                self.recv(k, dev(zh, x + step, 1 - c))
 
         def far(self):
             o = 1 - zh
-            self.recv(4, dev(o, x - sgn, c))
-            self.send(6, dev(o, x - sgn, c), ahead)
-            self.send(12, dev(o, x - sgn, c), mate)
-            self.recv(5, dev(o, x + sgn, c))
-            self.send(13, dev(o, x + sgn, c), mate)
-            self.recv(6, dev(o, x + 2, c))
-            self.send(14, dev(o, x + 2, c), mate)
-            self.recv(11, dev(o, x, 1 - c))
-            self.recv(12, dev(o, x + sgn, 1 - c))
-            self.recv(13, dev(o, x - sgn, 1 - c))
-            self.recv(14, dev(o, x + 2, 1 - c))
+            for k, step in ((4, -1), (5, 1), (6, 2)):
+                self.recv(k, dev(o, x + step, c))
+                self.send(8 + k, dev(o, x + step, c), mate)
+            for k, step in ((11, 0), (12, -1), (13, 1), (14, 2)):
+                self.recv(k, dev(o, x + step, 1 - c))
 
     phase("entry")
     barrier = pltpu.get_barrier_semaphore()
@@ -205,26 +196,38 @@
             barrier, inc=1, device_id=hdid(lax.rem(zl + k, 4), y), device_id_type=MESH
         )
 
+    loads = [
+        pltpu.make_async_copy(src, dst, local_sem.at[i])
+        for i, (src, dst) in enumerate(
+            [
+                (wzx_in, wzx_ref), (wbc_in, wbc_ref), (wdt_in, wdt_ref), (ids_in, ids_ref),
+                (hid_in, hid_ref), (gain_in, gain_ref), (cx_in, cx_ref), (cbc_in, cbc_ref),
+                (og_in, og_ref), (wout_in, wo.at[y]),
+            ]
+        )
+    ]
+    for load in loads:
+        load.start()
+
+    for load in loads[0:3]:
+        load.wait()
+    bc_t[:, 0:ROWS] = jnp.concatenate([wbc_ref[...], jnp.zeros((32, 256), F32)], axis=0).T[:, 0:ROWS]
+    sm_t[...] = jnp.zeros((32, 128), F32)
+    sm_t[0:16, 0:ROWS] = bc_t[pl.ds(pl.multiple_of(hd * 16, 16), 16), 0:ROWS]
+    sm_t[16:19, 0:ROWS] = wdt_ref[...]
+    small[dp] = sm_t[...].astype(BF16)
     zw = wzx_ref[:, 0, :]
     xw = wzx_ref[:, 1, :]
     wst[:, 0:128] = xw[:, 0:128]
     wst[:, 128:256] = jnp.concatenate([xw[:, 128:192], zw[:, 128:192]], axis=1)
     wst[:, 256:384] = zw[:, 0:128]
-    wst[:, 384:640] = wbc_ref[...]
     own_rows = pl.multiple_of(dp * ROWS, ROWS)
     w_buf[pl.ds(own_rows, ROWS), :] = wst[...].astype(BF16)
-    wdt_all[dp] = jnp.zeros((8, 128), F32)
-    wdt_all[dp, 0:HEADS, 0:ROWS] = wdt_ref[...]
 
     def w_rows(owner):
         return w_buf.at[pl.ds(pl.multiple_of(owner * ROWS, ROWS), ROWS), :]
 
-    def t_rows(owner):
-        return wdt_all.at[owner]
-
-    weights = Gather([(W_IDS, w_rows), (T_IDS, t_rows)])
-    own_copy = pltpu.make_async_copy(wout_ref, wo.at[y], local_sem)
-    own_copy.start()
+    weights = Gather([(W_IDS, w_rows)])
 
     @pl.when(dp == 0)
     def _():
@@ -242,16 +245,16 @@
 
     pl.semaphore_wait(barrier, DP - 1 + 6)
 
+    for k in (8, 7, 9, 6, 10, 5, 11, 12, 4, 13, 3, 14, 2, 15, 1):
+        send(T_IDS + k - 1, small.at[dp], small.at[dp], dpid(lax.rem(dp + k, DP)))
     weights.own()
+    for load in loads[3:9]:
+        load.wait()
     send(HALO, hid_ref.at[pl.ds(TOK - 16, 16), :], halo, dpid(lax.rem(dp + 1, DP)), dp < DP - 1)
 
     phase("ids")
     def wo_rows(y_, c_):
         return wo.at[lax.rem(y_ + 4, 4), pl.ds(pl.multiple_of(c_ * 96, 96), 96), :]
-
-    own_copy.wait()
-    for k in (1, 3, 2):
-        send(WO + k - 1, wo_rows(y, c), wo_rows(y, c), hdid(zl, lax.rem(y + k, 4)))
 
     own_ids = ids_ref[dp].astype(F32)
     prev_ids = ids_ref[jnp.maximum(dp - 1, 0)].astype(F32)
@@ -286,28 +289,20 @@
     nrm[0:16, :] = norm_rows(halo[...])
 
     phase("w_near")
-    weights.near()
-    phase("w_cross")
-    weights.cross()
-    phase("w_near_rest")
-    weights.near_rest()
-
-    phase("mm1")
-    k_half = D // 2
-    k_own = pl.multiple_of(zh * k_half, k_half)
-    k_far = pl.multiple_of((1 - zh) * k_half, k_half)
-    for n in range(0, 640, 128):
-        u_buf[:, n : n + 128] = dot(nrm[:, pl.ds(k_own, k_half)], w_buf[pl.ds(k_own, k_half), n : n + 128])
-
-    phase("w_far")
-    weights.far()
-
     phase("dt")
+    for k in range(1, DP):
+        owner = lax.rem(dp + DP - k, DP)
+        recv(T_IDS + k - 1, small.at[owner], dpid(owner))
     for j in range(DP):
-        rows = jnp.concatenate([wdt_all[j], jnp.zeros((120, 128), F32)], axis=0).T
+        rows = jnp.concatenate([small[j].astype(F32), jnp.zeros((96, 128), F32)], axis=0).T
         wdt_mat[ROWS * j : ROWS * j + ROWS, :] = rows[0:ROWS, :].astype(BF16)
-    dt_cols = dot(nrm[16:EXT, :], wdt_mat[...])
-    dt_rows = dt_cols.T[0:8, :].astype(BF16).astype(F32)
+    bc_cols = dot(nrm[...], wdt_mat[...])
+    bc_rows = jnp.concatenate([bc_cols[16:EXT, :].T, bc_cols[0:128, :].T], axis=1)
+    bc_parts[y, zl] = bc_rows[0:16, :].astype(BF16)
+    for k in (2, 1, 3):
+        zt = lax.rem(zl + k, 4)
+        send(BCZ + k - 1, bc_parts.at[y, zl], bc_parts.at[y, zl], hdid(zt, y))
+    dt_rows = bc_rows[16:24, 0:TOK].astype(BF16).astype(F32)
     sub = lax.broadcasted_iota(jnp.int32, (8, TOK), 0)
     lane = lax.broadcasted_iota(jnp.int32, (8, TOK), 1)
 
@@ -331,13 +326,53 @@
     to_end = jnp.exp(at_end - prefix) * step_rows
     cols[...] = jnp.concatenate([prefix, jnp.zeros((120, TOK), F32)], axis=0).T
 
+    phase("w_cross")
+    weights.cross()
+    phase("bcz")
+    for k in range(1, 4):
+        zs = lax.rem(zl + 4 - k, 4)
+        recv(BCZ + k - 1, bc_parts.at[y, zs], hdid(zs, y))
+    for k in (2, 1, 3):
+        send(BCY + k - 1, bc_parts.at[y], bc_parts.at[y], hdid(zl, lax.rem(y + k, 4)))
+
+    def wo_rows(y_, c_):
+        return wo.at[lax.rem(y_ + 4, 4), pl.ds(pl.multiple_of(c_ * 96, 96), 96), :]
+
+    loads[9].wait()
+    for k in (1, 3, 2):
+        send(WO + k - 1, wo_rows(y, c), wo_rows(y, c), hdid(zl, lax.rem(y + k, 4)))
+
+    phase("w_near_rest")
+    weights.near()
+    weights.near_rest()
+    phase("mm1")
+    k_half = D // 2
+    k_own = pl.multiple_of(zh * k_half, k_half)
+    k_far = pl.multiple_of((1 - zh) * k_half, k_half)
+    for n in range(0, 384, 128):
+        u_buf[:, n : n + 128] = dot(nrm[:, pl.ds(k_own, k_half)], w_buf[pl.ds(k_own, k_half), n : n + 128])
+
+    phase("bc_wait")
+    for k in range(1, 4):
+        ys = lax.rem(y + 4 - k, 4)
+        recv(BCY + k - 1, bc_parts.at[ys], hdid(zl, ys))
+    for half in range(2):
+        rows = jnp.concatenate(
+            [bc_parts[h % 4, h // 4].astype(F32) for h in range(8 * half, 8 * half + 8)], axis=0
+        )
+        col = 384 + 128 * half
+        u_buf[0:16, col : col + 128] = rows[:, TOK : TOK + 128].T[0:16, :]
+        u_buf[16:EXT, col : col + 128] = rows[:, 0:TOK].T
+
+    phase("w_far")
+    weights.far()
     phase("mm2")
-    for n in range(0, 640, 128):
+    for n in range(0, 384, 128):
         u_buf[:, n : n + 128] += dot(nrm[:, pl.ds(k_far, k_half)], w_buf[pl.ds(k_far, k_half), n : n + 128])
 
     phase("conv")
     for r in range(0, EXT, 176):
-        u_buf[r : r + 176, :] = u_buf[r : r + 176, :].astype(BF16).astype(F32)
+        u_buf[r : r + 176, 0:384] = u_buf[r : r + 176, 0:384].astype(BF16).astype(F32)
 
     for q in range(4):
         r = 128 * q
@@ -490,6 +525,21 @@
         xt = lax.rem(x + k, 4)
         send(TABX + k - 1, tabm.at[xt], tabx.at[k - 1], dpid(dev(zh, xt, c)))
 
+    phase("tabx_wait")
+    for k in range(1, 4):
+        recv(TABX + k - 1, tabx.at[k - 1], dpid(mate))
+    done = tabm[x].astype(F32)
+    for k in range(3):
+        done = done + tabx[k].astype(F32)
+    fin[dp // 2, pl.ds(my_half, 96), :] = done.astype(BF16)
+
+    def f_rows(owner):
+        return fin.at[owner // 2, pl.ds(pl.multiple_of(lax.rem(owner, 2) * 96, 96), 96), :]
+
+    phase("fin_own")
+    finals = Gather([(F_IDS, f_rows)])
+    finals.own()
+
     phase("wo_finish")
     for k in (1, 3, 2):
         recv(WO_MATE + k - 1, wo_rows(y - k, 1 - c), dpid(mate))
@@ -518,25 +568,10 @@
         zt = lax.rem(zl + k, 4)
         send(RSZ + k - 1, part.at[zt], rs_rx.at[k - 1], hdid(zt, y))
 
-    phase("tabx_wait")
-    for k in range(1, 4):
-        recv(TABX + k - 1, tabx.at[k - 1], dpid(mate))
-    done = tabm[x].astype(F32)
-    for k in range(3):
-        done = done + tabx[k].astype(F32)
-    fin[dp // 2, pl.ds(my_half, 96), :] = done.astype(BF16)
-
-    def f_rows(owner):
-        return fin.at[owner // 2, pl.ds(pl.multiple_of(lax.rem(owner, 2) * 96, 96), 96), :]
-
-    phase("fin_own")
-    finals = Gather([(F_IDS, f_rows)])
-    finals.own()
-
     phase("fin_near")
+    finals.cross()
+    phase("fin_cross")
     finals.near()
-    phase("fin_cross")
-    finals.cross()
     phase("fin_nearrest")
     finals.near_rest()
     phase("fin_far")
@@ -588,13 +623,25 @@
             jax.ShapeDtypeStruct((TOK // HD, D), BF16),
             jax.ShapeDtypeStruct((4, FEAT, NSTATE), BF16),
         ),
-        in_specs=[vmem, smem, smem, smem, smem] + [vmem] * 9,
+        in_specs=[smem] * 4 + [pl.BlockSpec(memory_space=pl.ANY)] * 10,
         out_specs=(vmem, vmem),
         scratch_shapes=[
-            pltpu.VMEM((D, 640), BF16),
-            pltpu.VMEM((ROWS, 640), F32),
-            pltpu.VMEM((DP, 8, 128), F32),
+            pltpu.VMEM((ROWS, 2, FEAT), F32),
+            pltpu.VMEM((ROWS, 256), F32),
+            pltpu.VMEM((HEADS, ROWS), F32),
+            pltpu.VMEM((DP, 4, 128), jnp.int32),
+            pltpu.VMEM((TOK, D), BF16),
+            pltpu.VMEM((D,), F32),
+            pltpu.VMEM((4, FEAT), F32),
+            pltpu.VMEM((4, 256), F32),
+            pltpu.VMEM((1, FEAT), F32),
+            pltpu.VMEM((D, 384), BF16),
+            pltpu.VMEM((ROWS, 384), F32),
+            pltpu.VMEM((256, 128), F32),
+            pltpu.VMEM((32, 128), F32),
+            pltpu.VMEM((DP, 32, 128), BF16),
             pltpu.VMEM((D, 128), BF16),
+            pltpu.VMEM((4, 4, 16, 640), BF16),
             pltpu.VMEM((16, D), BF16),
             pltpu.VMEM((EXT, D), BF16),
             pltpu.VMEM((EXT, 128), F32),
@@ -627,15 +674,16 @@
             pltpu.VMEM((3, 32, OUTW), BF16),
             pltpu.SemaphoreType.DMA((N_MSG,)),
             pltpu.SemaphoreType.DMA((N_MSG,)),
-            pltpu.SemaphoreType.DMA,
+            pltpu.SemaphoreType.DMA((10,)),
         ],
         compiler_params=pltpu.CompilerParams(
             collective_id=0, has_side_effects=True, vmem_limit_bytes=60 * 2**20
         ),
         name="layer",
     )(
-        token_prompt.reshape(DP, 4, 128), request_prompt, dt_bias, a_log, skip_gain, hidden,
-        in_gain, w_zx, w_bc, w_dt.T, conv_x, conv_bc, out_gain.reshape(1, FEAT), w_out,
+        request_prompt, dt_bias, a_log, skip_gain, w_zx, w_bc, w_dt.T,
+        token_prompt.reshape(DP, 4, 128), hidden, in_gain, conv_x, conv_bc,
+        out_gain.reshape(1, FEAT), w_out,
     )
     layer_out, states = pl.pallas_call(
         write_out,

time: 73.9 us -> 68.1 us (0.922)
  Pallas kernels: 72.8 us -> 67.3 us
    pallas_call x1, Pallas kernels: 71 us -> 65.6 us  [on_device(): pl.pallas_call(body, out_shape=(jax.ShapeDtypeStruct((TOK // HD, D), BF16...]
where the time goes in v3:
time: 68.1 us; the launch traced here: 68 us
  Pallas kernels  67.3 us (99%)
    pallas_call x1, Pallas kernels, on_device(): pl.pallas_call(body, out_shape=(jax.ShapeDtypeStruct((TOK // HD, D), BF16...  65.6 us
    pallas_call x1, Pallas kernels, on_device(): pl.pallas_call(write_out, out_shape=(jax.ShapeDtypeStruct((TOK // HD, D),...  1.76 us

profile of v3, /device:TPU:1, one launch (start us, length us, event | category | flops | bytes accessed | tf_op | source)
XLA Modules:
  0.0 68.0 jit_solution(545869883653033485)
XLA Ops:
  0.6 65.6 %layer.1 = (bf16[32,1536]{1,0:T(8,128)(2,1)}, bf16[4,192,128]{2,1,0:T(8,128)(2,1)}) custom-call(s32[4]{0:T(128)} %req_ref.1, f32[3]{0:T(128)} %dtb_ref.1, f32[3]{0:T(128)} %alog_ref.1, f32[3]{0:T(128)} %skip_ref.1, f32[96,2,192]{2,1,0:T(2,128)} %wzx_in.1, f32[96,256]{1,0:T(8,128)} %wbc_in.1, f32[3,96]{1,0:T(4,128)} %bitcast.5, s32[16,4,128]{2,1,0:T(4,128)} %bitcast.4, ...), custom_call_target="tpu_custom_call" | custom-call | tf_op jit(solution)/shard_map/layer/pallas_call | solution.py:620
  66.2 1.8 %write_out.1 = (bf16[32,1536]{1,0:T(8,128)(2,1)}, f32[4,192,128]{2,1,0:T(8,128)}) custom-call(bf16[32,1536]{1,0:T(8,128)(2,1)} %get-tuple-element.6.rows_ref, bf16[4,192,128]{2,1,0:T(8,128)(2,1)} %get-tuple-element.7.states_ref), custom_call_target="tpu_custom_call" | custom-call | tf_op jit(solution)/shard_map/write_out/pallas_call | solution.py:688

commit v4 on v3

--- a/solution.py
+++ b/solution.py
@@ -38,7 +38,8 @@
 RSZ = 72
 BCZ = 75
 BCY = 78
-N_MSG = 81
+TABC = 81
+N_MSG = 89
 
 
 def dot(a, b):
@@ -89,7 +90,7 @@
     cx_in, cbc_in, og_in, wout_in, out_ref, st_ref,
     wzx_ref, wbc_ref, wdt_ref, ids_ref, hid_ref, gain_ref, cx_ref, cbc_ref, og_ref,
     w_buf, wst, bc_t, sm_t, small, wdt_mat, bc_parts, halo, nrm, idc, u_buf, taps, x_t, x_b, b_b, c_b, b_all,
-    info_tx, info_rx, l_tx, l_rx, s_in, cols, smask, loc, tab0, tabs, tabz, tabm, tabx, fin,
+    info_tx, info_rx, l_tx, l_rx, s_in, cols, smask, loc, tab0, tabs, tabz, tabx, fin,
     g_send, a_rx, wo, part, own_acc, rs_rx, send_sem, recv_sem, local_sem,
 ):
     dp = lax.axis_index("dp")
@@ -232,6 +233,10 @@
     @pl.when(dp == 0)
     def _():
         halo[...] = jnp.zeros_like(halo)
+
+    @pl.when(x // 2 == zh)
+    def _():
+        tabz[...] = jnp.zeros_like(tabz)
 
     for j in range(4):
         @pl.when(dp < j + 1)
@@ -433,10 +438,6 @@
     mate_half = pl.multiple_of((1 - c) * 96, 96)
     send(TAB0, loc.at[:, pl.ds(mate_half, 96), :], tab0, dpid(mate))
 
-    phase("wo_mate")
-    for k in (1, 3, 2):
-        recv(WO + k - 1, wo_rows(y - k, c), dpid(mate))
-        send(WO_MATE + k - 1, wo_rows(y - k, c), wo_rows(y - k, c), dpid(mate))
     phase("scores")
     scol = lax.broadcasted_iota(jnp.int32, (128, TOK), 1)
     srow = lax.broadcasted_iota(jnp.int32, (128, TOK), 0)
@@ -463,8 +464,16 @@
     recv(TAB0, tab0, dpid(mate))
     for g in range(PROMPTS):
         tabs[g] = (loc[g, pl.ds(my_half, 96), :].astype(F32) + tab0[g].astype(F32)).astype(BF16)
-    send(TABZ, tabs.at[pl.ds(4 - 2 * zh, 2)], tabz, dpid(across))
-
+    for t in range(2):
+        send(TABC + 2 * x + t, tabs.at[4 - 2 * zh + t], tabz.at[x], dpid(dev(1 - zh, 2 * zh + t, c)))
+    for k in (2, 1, 3):
+        xt = lax.rem(x + k, 4)
+        send(TABX + k - 1, tabs.at[4 * zh + xt], tabx.at[k - 1], dpid(dev(zh, xt, c)))
+
+    phase("wo_mate")
+    for k in (1, 3, 2):
+        recv(WO + k - 1, wo_rows(y - k, c), dpid(mate))
+        send(WO_MATE + k - 1, wo_rows(y - k, c), wo_rows(y - k, c), dpid(mate))
     phase("state_wait")
     for j in range(4):
         recv(INFO_UP + j, info_rx.at[j], dpid(mate), dp >= j + 1)
@@ -516,21 +525,17 @@
         send(A2A + k - 1, g_send.at[:, yt], a_rx.at[y], hdid(zl, yt))
     a_rx[y] = g_send[:, y]
 
-    phase("tabz_wait")
-    recv(TABZ, tabz, dpid(across))
-    tabm[...] = tabs[pl.ds(4 * zh, 4)]
-    mid = 2 - 2 * zh
-    tabm[pl.ds(mid, 2)] = (tabs[pl.ds(4 * zh + mid, 2)].astype(F32) + tabz[...].astype(F32)).astype(BF16)
-    for k in range(1, 4):
-        xt = lax.rem(x + k, 4)
-        send(TABX + k - 1, tabm.at[xt], tabx.at[k - 1], dpid(dev(zh, xt, c)))
-
     phase("tabx_wait")
     for k in range(1, 4):
         recv(TABX + k - 1, tabx.at[k - 1], dpid(mate))
-    done = tabm[x].astype(F32)
+    shared = x // 2 == 1 - zh
+    for j in range(4):
+        recv(TABC + 2 * j + lax.rem(x, 2), tabz.at[j], dpid(mate), shared)
+    done = tabs[4 * zh + x].astype(F32)
     for k in range(3):
         done = done + tabx[k].astype(F32)
+    for j in range(4):
+        done = done + tabz[j].astype(F32)
     fin[dp // 2, pl.ds(my_half, 96), :] = done.astype(BF16)
 
     def f_rows(owner):
@@ -662,7 +667,6 @@
             pltpu.VMEM((PROMPTS, FEAT, NSTATE), BF16),
             pltpu.VMEM((PROMPTS, 96, NSTATE), BF16),
             pltpu.VMEM((PROMPTS, 96, NSTATE), BF16),
-            pltpu.VMEM((2, 96, NSTATE), BF16),
             pltpu.VMEM((4, 96, NSTATE), BF16),
             pltpu.VMEM((3, 96, NSTATE), BF16),
             pltpu.VMEM((PROMPTS, FEAT, NSTATE), BF16),

time: 68.1 us -> 61.8 us (0.907)
  Pallas kernels: 67.3 us -> 60.6 us
    pallas_call x1, Pallas kernels: 65.6 us -> 58.8 us  [on_device(): pl.pallas_call(body, out_shape=(jax.ShapeDtypeStruct((TOK // HD, D), BF16...]
where the time goes in v4:
time: 61.8 us; the launch traced here: 61.2 us
  Pallas kernels  60.6 us (98%)
  between operations  0.64 us (1%)
    pallas_call x1, Pallas kernels, on_device(): pl.pallas_call(body, out_shape=(jax.ShapeDtypeStruct((TOK // HD, D), BF16...  58.8 us
    pallas_call x1, Pallas kernels, on_device(): pl.pallas_call(write_out, out_shape=(jax.ShapeDtypeStruct((TOK // HD, D),...  1.76 us

profile of v4, /device:TPU:1, one launch (start us, length us, event | category | flops | bytes accessed | tf_op | source)
XLA Modules:
  0.0 61.2 jit_solution(18006164806064911740)
XLA Ops:
  0.6 58.8 %layer.1 = (bf16[32,1536]{1,0:T(8,128)(2,1)}, bf16[4,192,128]{2,1,0:T(8,128)(2,1)}) custom-call(s32[4]{0:T(128)} %req_ref.1, f32[3]{0:T(128)} %dtb_ref.1, f32[3]{0:T(128)} %alog_ref.1, f32[3]{0:T(128)} %skip_ref.1, f32[96,2,192]{2,1,0:T(2,128)} %wzx_in.1, f32[96,256]{1,0:T(8,128)} %wbc_in.1, f32[3,96]{1,0:T(4,128)} %bitcast.5, s32[16,4,128]{2,1,0:T(4,128)} %bitcast.4, ...), custom_call_target="tpu_custom_call" | custom-call | tf_op jit(solution)/shard_map/layer/pallas_call | solution.py:625
  59.5 1.8 %write_out.1 = (bf16[32,1536]{1,0:T(8,128)(2,1)}, f32[4,192,128]{2,1,0:T(8,128)}) custom-call(bf16[32,1536]{1,0:T(8,128)(2,1)} %get-tuple-element.6.rows_ref, bf16[4,192,128]{2,1,0:T(8,128)(2,1)} %get-tuple-element.7.states_ref), custom_call_target="tpu_custom_call" | custom-call | tf_op jit(solution)/shard_map/write_out/pallas_call | solution.py:692

commit v5 on v4

--- a/solution.py
+++ b/solution.py
@@ -410,10 +410,6 @@
             [x_t[64 * h : 64 * h + 64, :] * weight[h : h + 1, :] for h in range(HEADS)], axis=0
         ).astype(BF16)
 
-    l_tx[...] = dot(weighted_x(jnp.where(is_last, to_end, 0.0)), b_b[...]).astype(BF16)
-    for j in range(4):
-        send(STATE + j, l_tx, l_rx.at[j], dpid(lax.rem(dp + j + 1, DP)), dp + j + 1 < DP)
-
     phase("table_loc")
     def first_id(k):
         return ids_ref[jnp.clip(k, 0, DP - 1)][0:1, 0:1]
@@ -437,6 +433,10 @@
         loc[g] = dot(xw_end, b_all[:, 128 * g : 128 * g + 128]).astype(BF16)
     mate_half = pl.multiple_of((1 - c) * 96, 96)
     send(TAB0, loc.at[:, pl.ds(mate_half, 96), :], tab0, dpid(mate))
+
+    l_tx[...] = dot(weighted_x(jnp.where(is_last, to_end, 0.0)), b_b[...]).astype(BF16)
+    for j in range(4):
+        send(STATE + j, l_tx, l_rx.at[j], dpid(lax.rem(dp + j + 1, DP)), dp + j + 1 < DP)
 
     phase("scores")
     scol = lax.broadcasted_iota(jnp.int32, (128, TOK), 1)

time: 61.8 us -> 63.1 us (1.021)
  the two profiles are of different devices: /device:TPU:1 before, /device:TPU:194 now
where the time goes in v5:
time: 63.1 us; the launch traced here: 63 us
  Pallas kernels  62.4 us (99%)
  between operations  0.64 us (1%)
    pallas_call x1, Pallas kernels, on_device(): pl.pallas_call(body, out_shape=(jax.ShapeDtypeStruct((TOK // HD, D), BF16...  60.6 us
    pallas_call x1, Pallas kernels, on_device(): pl.pallas_call(write_out, out_shape=(jax.ShapeDtypeStruct((TOK // HD, D),...  1.76 us

profile of v5, /device:TPU:194, one launch (start us, length us, event | category | flops | bytes accessed | tf_op | source)
XLA Modules:
  0.0 63.0 jit_solution(10230478943647622596)
XLA Ops:
  0.6 60.6 %layer.1 = (bf16[32,1536]{1,0:T(8,128)(2,1)}, bf16[4,192,128]{2,1,0:T(8,128)(2,1)}) custom-call(s32[4]{0:T(128)} %req_ref.1, f32[3]{0:T(128)} %dtb_ref.1, f32[3]{0:T(128)} %alog_ref.1, f32[3]{0:T(128)} %skip_ref.1, f32[96,2,192]{2,1,0:T(2,128)} %wzx_in.1, f32[96,256]{1,0:T(8,128)} %wbc_in.1, f32[3,96]{1,0:T(4,128)} %bitcast.5, s32[16,4,128]{2,1,0:T(4,128)} %bitcast.4, ...), custom_call_target="tpu_custom_call" | custom-call | tf_op jit(solution)/shard_map/layer/pallas_call | solution.py:625
  61.2 1.8 %write_out.1 = (bf16[32,1536]{1,0:T(8,128)(2,1)}, f32[4,192,128]{2,1,0:T(8,128)}) custom-call(bf16[32,1536]{1,0:T(8,128)(2,1)} %get-tuple-element.6.rows_ref, bf16[4,192,128]{2,1,0:T(8,128)(2,1)} %get-tuple-element.7.states_ref), custom_call_target="tpu_custom_call" | custom-call | tf_op jit(solution)/shard_map/write_out/pallas_call | solution.py:692

commit v6 on v4

--- a/solution.py
+++ b/solution.py
@@ -298,6 +298,8 @@
     for k in range(1, DP):
         owner = lax.rem(dp + DP - k, DP)
         recv(T_IDS + k - 1, small.at[owner], dpid(owner))
+    phase("w_cross")
+    weights.cross()
     for j in range(DP):
         rows = jnp.concatenate([small[j].astype(F32), jnp.zeros((96, 128), F32)], axis=0).T
         wdt_mat[ROWS * j : ROWS * j + ROWS, :] = rows[0:ROWS, :].astype(BF16)
@@ -331,8 +333,6 @@
     to_end = jnp.exp(at_end - prefix) * step_rows
     cols[...] = jnp.concatenate([prefix, jnp.zeros((120, TOK), F32)], axis=0).T
 
-    phase("w_cross")
-    weights.cross()
     phase("bcz")
     for k in range(1, 4):
         zs = lax.rem(zl + 4 - k, 4)

time: 61.8 us -> 61.3 us (level)
  no operation moved by 1% of the time
where the time goes in v6:
time: 61.3 us; the launch traced here: 60.7 us
  Pallas kernels  60 us (98%)
  between operations  0.64 us (1%)
    pallas_call x1, Pallas kernels, on_device(): pl.pallas_call(body, out_shape=(jax.ShapeDtypeStruct((TOK // HD, D), BF16...  58.3 us
    pallas_call x1, Pallas kernels, on_device(): pl.pallas_call(write_out, out_shape=(jax.ShapeDtypeStruct((TOK // HD, D),...  1.76 us

profile of v6, /device:TPU:1, one launch (start us, length us, event | category | flops | bytes accessed | tf_op | source)
XLA Modules:
  0.0 60.7 jit_solution(9808936218724595900)
XLA Ops:
  0.6 58.3 %layer.1 = (bf16[32,1536]{1,0:T(8,128)(2,1)}, bf16[4,192,128]{2,1,0:T(8,128)(2,1)}) custom-call(s32[4]{0:T(128)} %req_ref.1, f32[3]{0:T(128)} %dtb_ref.1, f32[3]{0:T(128)} %alog_ref.1, f32[3]{0:T(128)} %skip_ref.1, f32[96,2,192]{2,1,0:T(2,128)} %wzx_in.1, f32[96,256]{1,0:T(8,128)} %wbc_in.1, f32[3,96]{1,0:T(4,128)} %bitcast.5, s32[16,4,128]{2,1,0:T(4,128)} %bitcast.4, ...), custom_call_target="tpu_custom_call" | custom-call | tf_op jit(solution)/shard_map/layer/pallas_call | solution.py:625
  58.9 1.8 %write_out.1 = (bf16[32,1536]{1,0:T(8,128)(2,1)}, f32[4,192,128]{2,1,0:T(8,128)}) custom-call(bf16[32,1536]{1,0:T(8,128)(2,1)} %get-tuple-element.6.rows_ref, bf16[4,192,128]{2,1,0:T(8,128)(2,1)} %get-tuple-element.7.states_ref), custom_call_target="tpu_custom_call" | custom-call | tf_op jit(solution)/shard_map/write_out/pallas_call | solution.py:692
